TPU v7x, 128 devices: a whole 4x4x4 slice. The times are simulated.
128 devices in a mesh: lat: 8 (over z_lo, x), lon: 16 (over y, z_hi, core).
Axes of the slice: x: 4, y: 4, z: 4 (z_hi: 2, z_lo: 2; z = z_hi * 2 + z_lo), core: 2. Of those that a mesh axis runs over, the one named last changes fastest.
Arguments:
- input_field: bfloat16 [1024, 1024, 128], P('lat', 'lon'), may hold values from -6 to 6
- conv_one: bfloat16 [3, 3, 128, 128], replicated, may hold values from -0.1875 to 0.1875
- conv_two: bfloat16 [3, 3, 128, 128], replicated, may hold values from -0.1875 to 0.1875
- merge_weight: bfloat16 [512, 512], replicated, may hold values from -0.25 to 0.25
- norm_gains: float32 [4, 512], replicated, may hold values from 0.1 to 1.9
- attention_in: bfloat16 [512, 1536], replicated, may hold values from -0.25 to 0.25
- attention_out: bfloat16 [512, 512], replicated, may hold values from -0.25 to 0.25
- dense_in: bfloat16 [512, 2048], replicated, may hold values from -0.25 to 0.25
- dense_out: bfloat16 [2048, 512], replicated, may hold values from -0.125 to 0.125
- expand_weight: bfloat16 [512, 512], replicated, may hold values from -0.25 to 0.25
Outputs:
- output_field: bfloat16 [1024, 1024, 128], P('lat', 'lon')
All inputs are finite; a program needn't handle non-finite values.
Results may differ from a plain program's by a relative error of at most 0.0095.
Values may be sent and summed in bfloat16 or wider, within the bound.
No kernel may reach another device: no remote copies, remote signals or barrier semaphores. Data moves between devices by JAX's collectives and lax.ppermute only.
A program may use at most 128 MiB of HBM per device.

v0:
```python
import functools
import math

import jax
import jax.numpy as jnp
from jax import lax
from jax.experimental import pallas as pl
from jax.experimental.pallas import tpu as pltpu
from jax.sharding import PartitionSpec as P

CHANNELS = 128
LATENT = 512
NUM_HEADS = 16
HEAD_WIDTH = 32
MLP_WIDTH = 2048
EPSILON = 1e-06
FLOOR = 0.75
GELU_ONE = math.sqrt(2.0 / math.pi)
GELU_TWO = GELU_ONE * 0.044715

ROWS, COLS = 128, 64
PAIRS = COLS // 2
STRIDE = 80
LEAD = 8
STAGE_ROWS = 28
FIRST_ROWS = 24
FIRST_STRIDE = 40
INNER, OUTER = (1, 2), (0, 3)
WINDOWS = 4
MIB = 1 << 20


def gelu(v):
    half = 0.5 * v
    return half + half * jnp.tanh(v * (GELU_ONE + GELU_TWO * (v * v)))


def front_kernel(blocks, keep_ref, x_ref, left_ref, right_ref, *rest):
    if blocks == OUTER:
        top_ref, bottom_ref = rest[:2]
        rest = rest[2:]
    w1_ref, w2_ref, wm_ref, out_ref, stage, sides, xab, firsts, fab = rest
    sides[0:2] = left_ref[...].astype(jnp.float32)
    sides[2:4] = right_ref[...].astype(jnp.float32)
    sub = lax.broadcasted_iota(jnp.int32, (16, 8, LATENT), 1)
    for at, block in enumerate(blocks):
        for p in range(2):
            start = 64 * p + 16 * block - 2
            low, high = max(start, 0), min(start + 20, ROWS)
            skip, count = low - start, min(start + 20, ROWS) - low

            def place(r, carry, p=p, low=low, skip=skip):
                to = pl.multiple_of((p * STAGE_ROWS + skip + r) * STRIDE + LEAD, 8)
                stage[pl.ds(to, COLS), :] = x_ref[low + r].astype(jnp.float32)
                return carry

            lax.fori_loop(0, count, place, 0, unroll=2)
            base = (p * STAGE_ROWS + skip) * STRIDE
            for c in range(2):
                stage[pl.ds(base + LEAD - 2 + c, count, stride=STRIDE), :] = sides[c, low:high, :]
                stage[pl.ds(base + LEAD + COLS + c, count, stride=STRIDE), :] = sides[
                    2 + c, low:high, :
                ]
            if skip > 0:
                for r in range(2):
                    to = (p * STAGE_ROWS + r) * STRIDE
                    stage[to : to + STRIDE, :] = top_ref[r].astype(jnp.float32)
            if skip + count < 20:
                for r in range(2):
                    to = (p * STAGE_ROWS + 18 + r) * STRIDE
                    stage[to : to + STRIDE, :] = bottom_ref[r].astype(jnp.float32)
        for p in range(2):
            for r in range(20):
                base = (p * STAGE_ROWS + r) * STRIDE + LEAD
                xab[p, r] = jnp.concatenate(
                    [stage[pl.ds(base + k, PAIRS, stride=2), :] for k in (-2, -1, 0, 1)], axis=-1
                ).astype(jnp.bfloat16)
        for p in range(2):
            for r0 in (0, 9):
                lhs = jnp.concatenate([xab[p, r0 + dy : r0 + dy + 9] for dy in range(3)], axis=-1)
                y = gelu(
                    jnp.dot(
                        lhs.reshape(9 * PAIRS, 1536),
                        w1_ref[...],
                        preferred_element_type=jnp.float32,
                    )
                )
                for r in range(9):
                    to = (p * FIRST_ROWS + r0 + r) * FIRST_STRIDE
                    for m in range(2):
                        firsts[m, to : to + PAIRS, :] = y[
                            r * PAIRS : (r + 1) * PAIRS, m * CHANNELS : (m + 1) * CHANNELS
                        ]
        lhs = jnp.concatenate(
            [
                jnp.concatenate(
                    [
                        stage[
                            pl.ds(
                                (p * STAGE_ROWS + dy) * STRIDE + LEAD + COLS - 2 + k,
                                FIRST_ROWS,
                                stride=STRIDE,
                            ),
                            :,
                        ]
                        for dy in range(3)
                        for k in range(4)
                    ],
                    axis=-1,
                )
                for p in range(2)
            ],
            axis=0,
        ).astype(jnp.bfloat16)
        edge = gelu(jnp.dot(lhs, w1_ref[...], preferred_element_type=jnp.float32))
        for p in range(2):
            base = p * FIRST_ROWS * FIRST_STRIDE
            mine = edge[p * FIRST_ROWS : (p + 1) * FIRST_ROWS]
            last = pl.ds(base + PAIRS, FIRST_ROWS, stride=FIRST_STRIDE)
            firsts[0, last, :] = mine[:, 0:CHANNELS]
            firsts[1, last, :] = mine[:, CHANNELS:] * keep_ref[1]
            begin = pl.ds(base, FIRST_ROWS, stride=FIRST_STRIDE)
            firsts[0, begin, :] = firsts[0, begin, :] * keep_ref[0]
        if block == 0:
            firsts[:, 0:FIRST_STRIDE, :] = firsts[:, 0:FIRST_STRIDE, :] * keep_ref[2]
        if block == 3:
            to = (FIRST_ROWS + 17) * FIRST_STRIDE
            firsts[:, to : to + FIRST_STRIDE, :] = firsts[:, to : to + FIRST_STRIDE, :] * keep_ref[3]
        for p in range(2):
            for r in range(18):
                base = (p * FIRST_ROWS + r) * FIRST_STRIDE
                fab[p, r] = jnp.concatenate(
                    [firsts[m, base + k : base + k + PAIRS, :] for k in range(2) for m in range(2)],
                    axis=-1,
                ).astype(jnp.bfloat16)
        for j in range(2):
            coarse = []
            for p in range(2):
                lhs = jnp.concatenate(
                    [fab[p, 8 * j + dy : 8 * j + dy + 8] for dy in range(3)], axis=-1
                )
                s = gelu(
                    jnp.dot(
                        lhs.reshape(8 * PAIRS, 1536),
                        w2_ref[...],
                        preferred_element_type=jnp.float32,
                    )
                ).astype(jnp.bfloat16)
                s = s.reshape(4, 2, PAIRS, 256)
                patches = jnp.concatenate([s[:, 0], s[:, 1]], axis=-1).reshape(4 * PAIRS, LATENT)
                coarse.append(
                    jnp.dot(patches, wm_ref[...], preferred_element_type=jnp.float32).reshape(
                        16, 8, LATENT
                    )
                )
            zero, one = coarse
            even = jnp.where(sub < 4, zero, pltpu.roll(one, 4, 1))
            odd = jnp.where(sub < 4, pltpu.roll(zero, 4, 1), one)
            u0 = 8 * at + 4 * j
            out_ref[u0 : u0 + 4, :, 0] = even.reshape(4, 4, 8, LATENT).astype(jnp.bfloat16)
            out_ref[u0 : u0 + 4, :, 1] = odd.reshape(4, 4, 8, LATENT).astype(jnp.bfloat16)


def front(blocks, keep, x, left, right, ends, w1, w2, wm):
    vmem = pl.BlockSpec(memory_space=pltpu.VMEM)
    args = (x, left, right) + tuple(ends) + (w1, w2, wm)
    out = pl.pallas_call(
        functools.partial(front_kernel, blocks),
        out_shape=jax.ShapeDtypeStruct((16, 4, 2, 8, LATENT), jnp.bfloat16),
        in_specs=[pl.BlockSpec(memory_space=pltpu.SMEM)] + [vmem] * len(args),
        out_specs=vmem,
        scratch_shapes=[
            pltpu.VMEM((2 * STAGE_ROWS * STRIDE, CHANNELS), jnp.float32),
            pltpu.VMEM((4, ROWS, CHANNELS), jnp.float32),
            pltpu.VMEM((2, 20, PAIRS, 512), jnp.bfloat16),
            pltpu.VMEM((2, 2 * FIRST_ROWS * FIRST_STRIDE, CHANNELS), jnp.float32),
            pltpu.VMEM((2, 18, PAIRS, 512), jnp.bfloat16),
        ],
        compiler_params=pltpu.CompilerParams(vmem_limit_bytes=28 * MIB),
        cost_estimate=pl.CostEstimate(
            flops=8_000_000_000, transcendentals=1_100_000, bytes_accessed=5_000_000
        ),
        name="front_inner" if blocks == INNER else "front_outer",
    )(keep, *args)
    return out.reshape(128, 8, LATENT)


def layer_norm(v, gain):
    center = v - jnp.mean(v, axis=-1, keepdims=True)
    spread = jnp.mean(center * center, axis=-1, keepdims=True)
    return center * lax.rsqrt(spread + EPSILON) * gain


def middle_kernel(
    tok_ref, gains_ref, qgain_ref, win_ref, wout_ref, wi_ref, wd_ref, out_ref, cells
):
    step = pl.program_id(0)

    @pl.when(step == 0)
    def _():
        held = tok_ref[...].reshape(128 * 8, LATENT).astype(jnp.float32)
        for q in range(4):
            cells[q] = held[:, q * 128 : (q + 1) * 128]

    places = [pl.ds(step + WINDOWS * p, 128, stride=8) for p in range(2)]
    tokens = jnp.concatenate(
        [jnp.concatenate([cells[q, place, :] for q in range(4)], axis=-1) for place in places],
        axis=0,
    )
    normed = layer_norm(tokens, gains_ref[0:1, :]).astype(jnp.bfloat16)
    projected = lax.dot_general(
        win_ref[...], normed, (((1,), (1,)), ((), ())), preferred_element_type=jnp.float32
    )

    def scaled(part):
        heads = part.reshape(NUM_HEADS, HEAD_WIDTH, 256)
        square = jnp.mean(heads * heads, axis=1, keepdims=True)
        return (heads * lax.rsqrt(jnp.maximum(square, FLOOR))).reshape(LATENT, 256)

    qgain = jnp.concatenate([qgain_ref[...], qgain_ref[...]], axis=-1)
    queries = (scaled(projected[0:LATENT]) * qgain).astype(jnp.bfloat16)
    keys = scaled(projected[LATENT : 2 * LATENT]).T.astype(jnp.bfloat16)
    values = projected[2 * LATENT :].astype(jnp.bfloat16)
    ones = jnp.ones((16, 256), jnp.bfloat16)
    blank = jnp.zeros((HEAD_WIDTH, 256), jnp.bfloat16)
    attended = []
    for h in range(NUM_HEADS):
        rows = slice(h * HEAD_WIDTH, (h + 1) * HEAD_WIDTH)
        group = h // 4
        right = jnp.concatenate([queries[rows] if i == h % 4 else blank for i in range(4)], axis=0)
        scores = jnp.dot(
            keys[:, group * 128 : (group + 1) * 128], right, preferred_element_type=jnp.float32
        )
        expon = jnp.exp2(scores).astype(jnp.bfloat16)
        both = jnp.dot(
            jnp.concatenate([values[rows], ones], axis=0), expon, preferred_element_type=jnp.float32
        )
        attended.append(both[0:HEAD_WIDTH] / both[HEAD_WIDTH : HEAD_WIDTH + 1])
    attended = jnp.concatenate(attended, axis=0).T.astype(jnp.bfloat16)
    mixed = (
        tokens + jnp.dot(attended, wout_ref[...], preferred_element_type=jnp.float32)
    ).astype(jnp.bfloat16).astype(jnp.float32)
    normed_two = layer_norm(mixed, gains_ref[3:4, :]).astype(jnp.bfloat16)
    updated = mixed
    for j in range(4):
        part = slice(j * 512, (j + 1) * 512)
        inner = gelu(
            jnp.dot(normed_two, wi_ref[:, part], preferred_element_type=jnp.float32)
        ).astype(jnp.bfloat16)
        updated = updated + jnp.dot(inner, wd_ref[part, :], preferred_element_type=jnp.float32)
    for p in range(2):
        for q in range(4):
            cells[q, places[p], :] = updated[128 * p : 128 * (p + 1), 128 * q : 128 * (q + 1)]

    @pl.when(step == WINDOWS - 1)
    def _():
        held = jnp.concatenate([cells[q] for q in range(4)], axis=-1)
        out_ref[...] = held.astype(jnp.bfloat16).reshape(128, 8, LATENT)


def middle(tokens, gains, qgain, win, wout, wi, wd):
    whole = lambda *shape: pl.BlockSpec(
        shape, lambda i: (0,) * len(shape), pipeline_mode=pl.Buffered(1)
    )
    return pl.pallas_call(
        middle_kernel,
        out_shape=jax.ShapeDtypeStruct((128, 8, LATENT), jnp.bfloat16),
        grid=(WINDOWS,),
        in_specs=[
            whole(128, 8, LATENT),
            whole(4, LATENT),
            whole(LATENT, 128),
            whole(3 * LATENT, LATENT),
            whole(LATENT, LATENT),
            whole(LATENT, MLP_WIDTH),
            whole(MLP_WIDTH, LATENT),
        ],
        out_specs=pl.BlockSpec((128, 8, LATENT), lambda i: (0, 0, 0)),
        scratch_shapes=[pltpu.VMEM((4, 1024, 128), jnp.float32)],
        compiler_params=pltpu.CompilerParams(vmem_limit_bytes=32 * MIB),
        cost_estimate=pl.CostEstimate(
            flops=16_000_000_000, transcendentals=6_000_000, bytes_accessed=9_000_000
        ),
        name="middle",
    )(tokens, gains, qgain, win, wout, wi, wd)


def back_kernel(cells_ref, x_ref, we_ref, *rest):
    out_ref, even, odd = rest[-3:]
    expanded = jnp.dot(
        cells_ref[...].reshape(512, LATENT), we_ref[...], preferred_element_type=jnp.float32
    )
    for di, held in enumerate((even, odd)):
        for dj in range(2):
            lanes = (2 * di + dj) * CHANNELS
            held[pl.ds(dj, 512, stride=2), :] = expanded[:, lanes : lanes + CHANNELS]
    for di, held in enumerate((even, odd)):
        for u in range(8):
            rows = held[u * 128 : (u + 1) * 128, :].reshape(8, 2, 8, CHANNELS)
            for p in range(2):
                fine = rows[:, p].reshape(COLS, CHANNELS)
                old = x_ref[p, 2 * u + di].astype(jnp.float32)
                out_ref[p, 2 * u + di] = (fine + old).astype(jnp.bfloat16)


def back(blocks, cells, x, we, before):
    step = blocks[1] - blocks[0]
    fine = pl.BlockSpec((2, 16, COLS, CHANNELS), lambda i: (0, blocks[0] + step * i, 0, 0))
    specs = [
        pl.BlockSpec((64, 8, LATENT), lambda i: (i, 0, 0)),
        fine,
        pl.BlockSpec((LATENT, LATENT), lambda i: (0, 0), pipeline_mode=pl.Buffered(1)),
    ]
    args = (cells, x, we)
    aliases = {}
    if before is not None:
        specs.append(pl.BlockSpec(memory_space=pl.ANY))
        args += (before,)
        aliases = {3: 0}
    return pl.pallas_call(
        back_kernel,
        out_shape=jax.ShapeDtypeStruct((2, 64, COLS, CHANNELS), jnp.bfloat16),
        grid=(2,),
        in_specs=specs,
        out_specs=fine,
        scratch_shapes=[pltpu.VMEM((1024, CHANNELS), jnp.float32)] * 2,
        input_output_aliases=aliases,
        compiler_params=pltpu.CompilerParams(vmem_limit_bytes=20 * MIB),
        cost_estimate=pl.CostEstimate(
            flops=540_000_000, transcendentals=0, bytes_accessed=4_000_000
        ),
        name="back_inner" if blocks == INNER else "back_outer",
    )(*args)


def paired(kernel):
    none = ((0, 0), (0, 0), (0, 0))
    return jnp.concatenate(
        [
            jnp.pad(kernel, (none[0], (0, 1), none[1], none[2])),
            jnp.pad(kernel, (none[0], (1, 0), none[1], none[2])),
        ],
        axis=-1,
    ).reshape(1536, 256)


def from_before(cells, axis):
    ends = lax.axis_size(axis) - 1
    return lax.ppermute(cells, axis, [(i, i + 1) for i in range(ends)])


def from_after(cells, axis):
    ends = lax.axis_size(axis) - 1
    return lax.ppermute(cells, axis, [(i + 1, i) for i in range(ends)])


def per_device(
    x,
    conv_one,
    conv_two,
    merge_weight,
    norm_gains,
    attention_in,
    attention_out,
    dense_in,
    dense_out,
    expand_weight,
):
    lat, lon = lax.axis_index("lat"), lax.axis_index("lon")
    keep = jnp.stack(
        [lon > 0, lon < lax.axis_size("lon") - 1, lat > 0, lat < lax.axis_size("lat") - 1]
    ).astype(jnp.float32)
    left = from_before(x[:, COLS - 2 :, :].transpose(1, 0, 2), "lon")
    right = from_after(x[:, :2, :].transpose(1, 0, 2), "lon")
    w1, w2 = paired(conv_one), paired(conv_two)
    win = attention_in.T
    scale = HEAD_WIDTH**-0.5 * math.log2(math.e)
    qgain = jnp.broadcast_to(
        (norm_gains[1] * norm_gains[2] * scale)[:, None], (LATENT, 128)
    )

    def wide(rows):
        return jnp.concatenate(
            [
                jnp.zeros((2, LEAD - 2, CHANNELS), jnp.bfloat16),
                left[:, rows].transpose(1, 0, 2),
                x[rows],
                right[:, rows].transpose(1, 0, 2),
                jnp.zeros((2, STRIDE - LEAD - COLS - 2, CHANNELS), jnp.bfloat16),
            ],
            axis=1,
        )

    top = from_before(wide(slice(ROWS - 2, ROWS)), "lat")
    bottom = from_after(wide(slice(0, 2)), "lat")
    exchange = functools.partial(
        lax.all_to_all, axis_name=("lat", "lon"), split_axis=0, concat_axis=0, tiled=True
    )
    inner = front(INNER, keep, x, left, right, (), w1, w2, merge_weight)
    inner = exchange(inner)
    outer = front(OUTER, keep, x, left, right, (top, bottom), w1, w2, merge_weight)
    outer = exchange(outer)
    weights = (norm_gains, qgain, win, attention_out, dense_in, dense_out)
    inner = exchange(middle(inner, *weights))
    outer = exchange(middle(outer, *weights))
    field = x.reshape(2, 64, COLS, CHANNELS)
    result = back(INNER, inner, field, expand_weight, None)
    result = back(OUTER, outer, field, expand_weight, result)
    return result.reshape(ROWS, COLS, CHANNELS)


def solution(mesh):
    return jax.shard_map(
        per_device,
        mesh=mesh,
        in_specs=(P("lat", "lon", None), P(), P(), P(), P(), P(), P(), P(), P(), P()),
        out_specs=P("lat", "lon", None),
        check_vma=False,
    )
```

profile of v0, /device:TPU:1, one launch (start us, length us, event | category | flops | bytes accessed | tf_op | source)
XLA Modules:
  0.0 182.0 jit_solution(1741770317313859011)
XLA Ops:
  0.0 1.3 fusion.7
  1.3 6.9 %collective-permute-start = (bf16[2,128,128]{2,1,0:T(8,128)(2,1)S(1)}, bf16[2,128,128]{2,1,0:T(8,128)(2,1)S(1)}, u32[]{:S(2)}, u32[]{:S(2)}) collective-permute-start(bf16[2,128,128]{2,1,0:T(8,128)(2,1)S(1)} %bitcast.36), channel_id=1, source_target_pairs={{0,1},{1,2},{2,3},{3,4},{4,5},{5,6},{6,7},{7,8},{8,9},{9,10},{10,1... | collective-permute-start | bytes 196616 | tf_op jit(solution)/shard_map/ppermute | solution.py:349
  8.2 1.9 %collective-permute-start.1 = (bf16[2,128,128]{2,1,0:T(8,128)(2,1)S(1)}, bf16[2,128,128]{2,1,0:T(8,128)(2,1)S(1)}, u32[]{:S(2)}, u32[]{:S(2)}) collective-permute-start(bf16[2,128,128]{2,1,0:T(8,128)(2,1)S(1)} %bitcast.37), channel_id=1, source_target_pairs={{1,0},{2,1},{3,2},{4,3},{5,4},{6,5},{7,6},{8,7},{9,8},{10,9},{11,1... | collective-permute-start | bytes 196616 | tf_op jit(solution)/shard_map/ppermute | solution.py:354
  10.2 0.8 fusion.6
  11.0 1.2 fusion.4
  12.1 0.0 copy-start.11
  12.1 1.4 fusion.5
  13.6 0.0 copy-start.13
  13.6 0.1 add_convert_fusion.keep_ref
  13.6 0.0 collective-permute-done.left_ref
  13.7 1.7 collective-permute-done.1.right_ref
  15.3 0.0 copy-done
  15.3 0.0 copy-done.20
  15.3 9.1 %front_inner.1 = bf16[16,4,2,8,512]{4,3,2,1,0:T(8,128)(2,1)S(1)} custom-call(f32[4]{0:T(128)S(1)} %add_convert_fusion.keep_ref, bf16[128,64,128]{2,1,0:T(8,128)(2,1)S(1)} %copy-done, bf16[2,128,128]{2,1,0:T(8,128)(2,1)S(1)} %collective-permute-done.left_ref, bf16[2,128,128]{2,1,0:T(8,128)(2,1)S(1)} %collective-permute-done.1.right_ref, ...), custom_call_target="tpu_custom_call" | custom-call | flops 8000000000 | bytes 5000000 | tf_op jit(solution)/shard_map/front_inner/pallas_call | solution.py:167
  24.5 0.0 copy-done.11
  24.5 0.0 copy-done.13
  24.5 0.0 copy-start.7
  24.5 1.0 copy-done.7
  25.5 8.4 %all-to-all-start.2 = ((bf16[128,8,512]{2,1,0:T(8,128)(2,1)}), bf16[128,8,512]{2,1,0:T(8,128)(2,1)S(1)}, u32[]{:S(2)}, u32[]{:S(2)}) async-start(bf16[128,8,512]{2,1,0:T(8,128)(2,1)} %bitcast.30), calls=%async_computation.2 | async-start | bytes 2097152 | tf_op jit(solution)/shard_map/all_to_all | solution.py:400
  34.0 0.1 concatenate.13
  34.0 1.3 collective-permute-start.3
  35.3 0.1 concatenate.12
  35.4 4.2 %collective-permute-start.2 = (bf16[2,80,128]{2,1,0:T(8,128)(2,1)S(1)}, bf16[2,80,128]{2,1,0:T(8,128)(2,1)S(1)}, u32[]{:S(2)}, u32[]{:S(2)}) collective-permute-start(bf16[2,80,128]{2,1,0:T(8,128)(2,1)S(1)} %concatenate.12), channel_id=1, source_target_pairs={{0,16},{16,32},{32,48},{48,64},{64,80},{80,96},{96,112},{1,17},{17... | collective-permute-start | bytes 122888 | tf_op jit(solution)/shard_map/ppermute | solution.py:349
  39.6 0.0 copy-done.15
  39.6 2.6 %copy.18 = bf16[512,1536]{0,1:T(8,128)(2,1)} copy(bf16[512,1536]{1,0:T(8,128)(2,1)} %param.15) | data formatting | bytes 3145728 | tf_op args[5]
  42.2 5.3 %collective-permute-done.3.rest_1_ = bf16[2,80,128]{2,1,0:T(8,128)(2,1)S(1)} collective-permute-done((bf16[2,80,128]{2,1,0:T(8,128)(2,1)S(1)}, bf16[2,80,128]{2,1,0:T(8,128)(2,1)S(1)}, u32[]{:S(2)}, u32[]{:S(2)}) %collective-permute-start.3) | collective-permute-done | bytes 40992 | tf_op jit(solution)/shard_map/ppermute | solution.py:354
  47.5 0.0 collective-permute-done.2.rest_0_
  47.5 1.1 copy-done.12
  48.6 1.1 copy-done.14
  49.8 1.0 copy-done.21
  50.8 9.1 %front_outer.1 = bf16[16,4,2,8,512]{4,3,2,1,0:T(8,128)(2,1)S(1)} custom-call(f32[4]{0:T(128)S(1)} %add_convert_fusion.keep_ref, bf16[128,64,128]{2,1,0:T(8,128)(2,1)S(1)} %copy-done, bf16[2,128,128]{2,1,0:T(8,128)(2,1)S(1)} %collective-permute-done.left_ref, bf16[2,128,128]{2,1,0:T(8,128)(2,1)S(1)} %collective-permute-done.1.right_ref, ...), custom_call_target="tpu_custom_call" | custom-call | flops 8000000000 | bytes 5000000 | tf_op jit(solution)/shard_map/front_outer/pallas_call | solution.py:167
  59.9 0.0 copy-start.8
  59.9 1.0 copy-done.8
  60.9 0.0 all-to-all-done.2.tok_ref
  60.9 10.6 %all-to-all-start = ((bf16[128,8,512]{2,1,0:T(8,128)(2,1)}), bf16[128,8,512]{2,1,0:T(8,128)(2,1)}, u32[]{:S(2)}, u32[]{:S(2)}) async-start(bf16[128,8,512]{2,1,0:T(8,128)(2,1)} %bitcast.31), calls=%async_computation | async-start | bytes 2097152 | tf_op jit(solution)/shard_map/all_to_all | solution.py:402
  71.5 0.1 broadcast_in_dim.2.qgain_ref
  71.7 0.0 copy-start.5
  71.7 1.4 copy-done.5
  73.1 1.6 copy-done.16
  74.7 1.6 copy-done.18
  76.3 1.0 copy-done.22
  77.3 26.7 %middle.3 = bf16[128,8,512]{2,1,0:T(8,128)(2,1)S(1)} custom-call(bf16[128,8,512]{2,1,0:T(8,128)(2,1)S(1)} %all-to-all-done.2.tok_ref, f32[4,512]{1,0:T(4,128)S(1)} %copy-done.15, f32[512,128]{1,0:T(8,128)S(1)} %broadcast_in_dim.2.qgain_ref, bf16[1536,512]{1,0:T(8,128)(2,1)S(1)} %bitcast.28, bf16[512,512]{1,0:T(8,128)(2,1)S(1)} %copy-done.22, ...), custom_call_target="tpu_custom_call" | custom-call | flops 16000000000 | bytes 9000000 | tf_op jit(solution)/shard_map/middle/pallas_call | solution.py:265
  104.1 0.0 copy-start.9
  104.1 1.0 copy-done.9
  105.0 0.0 all-to-all-done.tok_ref
  105.0 9.8 %all-to-all-start.3 = ((bf16[128,8,512]{2,1,0:T(8,128)(2,1)}), bf16[128,8,512]{2,1,0:T(8,128)(2,1)S(1)}, u32[]{:S(2)}, u32[]{:S(2)}) async-start(bf16[128,8,512]{2,1,0:T(8,128)(2,1)} %copy-done.9), calls=%async_computation.3 | async-start | bytes 2097152 | tf_op jit(solution)/shard_map/all_to_all | solution.py:404
  114.8 0.0 copy-start.6
  114.8 1.4 copy-done.6
  116.2 1.6 copy-done.17
  117.8 1.6 copy-done.19
  119.4 1.0 copy-done.23
  120.4 27.9 %middle.2 = bf16[128,8,512]{2,1,0:T(8,128)(2,1)S(1)} custom-call(bf16[128,8,512]{2,1,0:T(8,128)(2,1)} %all-to-all-done.tok_ref, f32[4,512]{1,0:T(4,128)S(1)} %copy-done.15, f32[512,128]{1,0:T(8,128)S(1)} %broadcast_in_dim.2.qgain_ref, bf16[1536,512]{1,0:T(8,128)(2,1)S(1)} %bitcast.29, bf16[512,512]{1,0:T(8,128)(2,1)S(1)} %copy-done.23, ...), custom_call_target="tpu_custom_call" | custom-call | flops 16000000000 | bytes 9000000 | tf_op jit(solution)/shard_map/middle/pallas_call | solution.py:265
  148.4 0.0 copy-start.10
  148.4 1.0 copy-done.10
  149.4 0.0 all-to-all-done.3.cells_ref
  149.4 1.0 copy-done.1
  150.4 9.8 %all-to-all-start.1 = ((bf16[128,8,512]{2,1,0:T(8,128)(2,1)}), bf16[128,8,512]{2,1,0:T(8,128)(2,1)S(1)}, u32[]{:S(2)}, u32[]{:S(2)}) async-start(bf16[128,8,512]{2,1,0:T(8,128)(2,1)} %copy-done.10), calls=%async_computation.1 | async-start | bytes 2097152 | tf_op jit(solution)/shard_map/all_to_all | solution.py:405
  160.1 0.0 copy-start.2
  160.1 1.2 copy-done.2
  161.4 1.0 copy-done.3
  162.4 1.9 %back_inner.1.rest_0_ = bf16[2,64,64,128]{3,2,1,0:T(8,128)(2,1)} custom-call(bf16[128,8,512]{2,1,0:T(8,128)(2,1)S(1)} %copy-done.2, bf16[2,64,64,128]{3,2,1,0:T(8,128)(2,1)S(1)} %bitcast.26, bf16[512,512]{1,0:T(8,128)(2,1)S(1)} %copy-done.3), custom_call_target="tpu_custom_call" | custom-call | flops 540000000 | bytes 4000000 | tf_op jit(solution)/shard_map/back_inner/pallas_call | solution.py:320
  164.3 14.8 %all-to-all-done.1.cells_ref = bf16[128,8,512]{2,1,0:T(8,128)(2,1)S(1)} async-done(((bf16[128,8,512]{2,1,0:T(8,128)(2,1)}), bf16[128,8,512]{2,1,0:T(8,128)(2,1)S(1)}, u32[]{:S(2)}, u32[]{:S(2)}) %all-to-all-start.1) | async-done | bytes 1048608 | tf_op jit(solution)/shard_map/all_to_all | solution.py:405
  179.1 1.0 copy-done.4
  180.1 1.9 %back_outer.1 = bf16[2,64,64,128]{3,2,1,0:T(8,128)(2,1)} custom-call(bf16[128,8,512]{2,1,0:T(8,128)(2,1)S(1)} %all-to-all-done.1.cells_ref, bf16[2,64,64,128]{3,2,1,0:T(8,128)(2,1)S(1)} %bitcast.27, bf16[512,512]{1,0:T(8,128)(2,1)S(1)} %copy-done.4, bf16[2,64,64,128]{3,2,1,0:T(8,128)(2,1)} %back_inner.1.rest_0_), custom_call_target="tpu_custom_call", output_to_operand_aliasing={{}: (3, {})} | custom-call | flops 540000000 | bytes 4000000 | tf_op jit(solution)/shard_map/back_outer/pallas_call | solution.py:320
  (25 shorter events, 0.1 us)
Async XLA Ops:
  0.0 15.3 %copy-start = (bf16[128,64,128]{2,1,0:T(8,128)(2,1)S(1)}, bf16[128,64,128]{2,1,0:T(8,128)(2,1)}, u32[]{:S(2)}) copy-start(bf16[128,64,128]{2,1,0:T(8,128)(2,1)} %x_ref.3) | copy-start | bytes 6291460
  1.3 12.3 %collective-permute-start = (bf16[2,128,128]{2,1,0:T(8,128)(2,1)S(1)}, bf16[2,128,128]{2,1,0:T(8,128)(2,1)S(1)}, u32[]{:S(2)}, u32[]{:S(2)}) collective-permute-start(bf16[2,128,128]{2,1,0:T(8,128)(2,1)S(1)} %bitcast.36), channel_id=1, source_target_pairs={{0,1},{1,2},{2,3},{3,4},{4,5},{5,6},{6,7},{7,8},{8,9},{9,10},{10,1... | collective-permute-start | bytes 196616 | tf_op jit(solution)/shard_map/ppermute | solution.py:349
  8.2 7.1 %collective-permute-start.1 = (bf16[2,128,128]{2,1,0:T(8,128)(2,1)S(1)}, bf16[2,128,128]{2,1,0:T(8,128)(2,1)S(1)}, u32[]{:S(2)}, u32[]{:S(2)}) collective-permute-start(bf16[2,128,128]{2,1,0:T(8,128)(2,1)S(1)} %bitcast.37), channel_id=1, source_target_pairs={{1,0},{2,1},{3,2},{4,3},{5,4},{6,5},{7,6},{8,7},{9,8},{10,9},{11,1... | collective-permute-start | bytes 196616 | tf_op jit(solution)/shard_map/ppermute | solution.py:354
  11.0 4.4 %copy-start.20 = (bf16[512,512]{1,0:T(8,128)(2,1)S(1)}, bf16[512,512]{1,0:T(8,128)(2,1)}, u32[]{:S(2)}) copy-start(bf16[512,512]{1,0:T(8,128)(2,1)} %rest_2_.1) | copy-start | bytes 1572868
  12.1 12.3 %copy-start.11 = (bf16[3,4,128,256]{3,2,1,0:T(8,128)(2,1)}, bf16[3,4,128,256]{3,2,1,0:T(8,128)(2,1)S(1)}, u32[]{:S(2)}) copy-start(bf16[3,4,128,256]{3,2,1,0:T(8,128)(2,1)S(1)} %fusion.4) | copy-start | bytes 2359300
  13.6 10.9 %copy-start.13 = (bf16[3,4,128,256]{3,2,1,0:T(8,128)(2,1)}, bf16[3,4,128,256]{3,2,1,0:T(8,128)(2,1)S(1)}, u32[]{:S(2)}) copy-start(bf16[3,4,128,256]{3,2,1,0:T(8,128)(2,1)S(1)} %fusion.5) | copy-start | bytes 2359300
  24.5 1.0 copy-start.7
  25.5 14.1 %copy-start.15 = (f32[4,512]{1,0:T(4,128)S(1)}, f32[4,512]{1,0:T(4,128)}, u32[]{:S(2)}) copy-start(f32[4,512]{1,0:T(4,128)} %gains_ref.3) | copy-start | bytes 24580
  25.5 35.4 %all-to-all-start.2 = ((bf16[128,8,512]{2,1,0:T(8,128)(2,1)}), bf16[128,8,512]{2,1,0:T(8,128)(2,1)S(1)}, u32[]{:S(2)}, u32[]{:S(2)}) async-start(bf16[128,8,512]{2,1,0:T(8,128)(2,1)} %bitcast.30), calls=%async_computation.2 | async-start | bytes 2097152 | tf_op jit(solution)/shard_map/all_to_all | solution.py:400
  34.0 13.4 %collective-permute-start.3 = (bf16[2,80,128]{2,1,0:T(8,128)(2,1)S(1)}, bf16[2,80,128]{2,1,0:T(8,128)(2,1)S(1)}, u32[]{:S(2)}, u32[]{:S(2)}) collective-permute-start(bf16[2,80,128]{2,1,0:T(8,128)(2,1)S(1)} %concatenate.13), channel_id=1, source_target_pairs={{16,0},{32,16},{48,32},{64,48},{80,64},{96,80},{112,96},{17,1},{33... | collective-permute-start | bytes 122888 | tf_op jit(solution)/shard_map/ppermute | solution.py:354
  35.4 12.1 %collective-permute-start.2 = (bf16[2,80,128]{2,1,0:T(8,128)(2,1)S(1)}, bf16[2,80,128]{2,1,0:T(8,128)(2,1)S(1)}, u32[]{:S(2)}, u32[]{:S(2)}) collective-permute-start(bf16[2,80,128]{2,1,0:T(8,128)(2,1)S(1)} %concatenate.12), channel_id=1, source_target_pairs={{0,16},{16,32},{32,48},{48,64},{64,80},{80,96},{96,112},{1,17},{17... | collective-permute-start | bytes 122888 | tf_op jit(solution)/shard_map/ppermute | solution.py:349
  47.5 1.1 copy-start.12
  48.6 1.1 copy-start.14
  49.8 1.0 copy-start.21
  59.9 1.0 copy-start.8
  60.9 44.1 %all-to-all-start = ((bf16[128,8,512]{2,1,0:T(8,128)(2,1)}), bf16[128,8,512]{2,1,0:T(8,128)(2,1)}, u32[]{:S(2)}, u32[]{:S(2)}) async-start(bf16[128,8,512]{2,1,0:T(8,128)(2,1)} %bitcast.31), calls=%async_computation | async-start | bytes 2097152 | tf_op jit(solution)/shard_map/all_to_all | solution.py:402
  71.7 1.4 copy-start.5
  73.1 1.6 copy-start.16
  74.7 1.6 copy-start.18
  76.3 1.0 copy-start.22
  104.1 1.0 copy-start.9
  105.0 44.4 %all-to-all-start.3 = ((bf16[128,8,512]{2,1,0:T(8,128)(2,1)}), bf16[128,8,512]{2,1,0:T(8,128)(2,1)S(1)}, u32[]{:S(2)}, u32[]{:S(2)}) async-start(bf16[128,8,512]{2,1,0:T(8,128)(2,1)} %copy-done.9), calls=%async_computation.3 | async-start | bytes 2097152 | tf_op jit(solution)/shard_map/all_to_all | solution.py:404
  114.8 1.4 copy-start.6
  116.2 1.6 copy-start.17
  117.8 1.6 copy-start.19
  119.4 1.0 copy-start.23
  148.4 1.0 copy-start.10
  149.4 1.0 copy-start.1
  150.4 28.7 %all-to-all-start.1 = ((bf16[128,8,512]{2,1,0:T(8,128)(2,1)}), bf16[128,8,512]{2,1,0:T(8,128)(2,1)S(1)}, u32[]{:S(2)}, u32[]{:S(2)}) async-start(bf16[128,8,512]{2,1,0:T(8,128)(2,1)} %copy-done.10), calls=%async_computation.1 | async-start | bytes 2097152 | tf_op jit(solution)/shard_map/all_to_all | solution.py:405
  160.1 1.2 copy-start.2
  161.4 1.0 copy-start.3
  179.1 1.0 copy-start.4
where the time goes:
time: 183 us; the launch traced here: 182 us
  Pallas kernels  76.7 us (42%)
  starting transfers between devices  52.8 us (29%)
  local copies, waits for them, and re-layouts  27.7 us (15%)
  waiting for transfers between devices  21.7 us (12%)
  other arithmetic  2.66 us (1%)
    pallas_call x2, Pallas kernels, middle(): pl.pallas_call(middle_kernel, out_shape=jax.ShapeDtypeStruct((128, 8, LAT...  54.7 us
    unnamed x51, local copies, waits for them, and re-layouts  25.4 us
    pallas_call x2, Pallas kernels, front(): pl.pallas_call(functools.partial(front_kernel, blocks), out_shape=jax.Sha...  18.2 us
    all_to_all x1, waiting for transfers between devices, per_device(): outer = exchange(middle(outer, *weights))  14.8 us
    ppermute x2, starting transfers between devices, from_before(): return lax.ppermute(cells, axis, [(i, i + 1) for i in range(ends)])  11.1 us
    all_to_all x1, starting transfers between devices, per_device(): outer = exchange(outer)  10.6 us
    all_to_all x1, starting transfers between devices, per_device(): inner = exchange(middle(inner, *weights))  9.76 us
    all_to_all x1, starting transfers between devices, per_device(): outer = exchange(middle(outer, *weights))  9.76 us
  transfers between devices with their start and end apart: 8, of which 3 were waited for; matrix products, arithmetic and copies ran while one was open for 3% of the time, Pallas kernels for 36%

commit v1 on v0

v1 whole, which is shorter than its diff:
```python
import functools
import math

import jax
import jax.numpy as jnp
from jax import lax
from jax.experimental import pallas as pl
from jax.experimental.pallas import tpu as pltpu
from jax.sharding import PartitionSpec as P

CHANNELS = 128
LATENT = 512
NUM_HEADS = 16
HEAD_WIDTH = 32
MLP_WIDTH = 2048
EPSILON = 1e-06
FLOOR = 0.75
GELU_ONE = math.sqrt(2.0 / math.pi)
GELU_TWO = GELU_ONE * 0.044715

ROWS, COLS = 128, 64
PAIRS = COLS // 2
STRIDE = 80
LEAD = 8
STAGE_ROWS = 28
FIRST_ROWS = 24
FIRST_STRIDE = 40
INNER, OUTER = (1, 2), (0, 3)
WINDOWS = 4
MLP_ROWS = 512
MLP_PART = 256
GROUP = 4
CONV_ONE, CONV_TWO, MERGE = 9, 8, 8
LIMIT = 60 << 20


def gelu(v):
    half = 0.5 * v
    return half + half * jnp.tanh(v * (GELU_ONE + GELU_TWO * (v * v)))


def pair_columns(kernel_ref, out_ref):
    for dy in range(3):
        for k in range(4):
            for m in range(2):
                inside = 0 <= k - m <= 2
                if inside == (kernel_ref is None):
                    continue
                rows = slice((4 * dy + k) * CHANNELS, (4 * dy + k + 1) * CHANNELS)
                lanes = slice(m * CHANNELS, (m + 1) * CHANNELS)
                if inside:
                    out_ref[rows, lanes] = kernel_ref[dy, k - m]
                else:
                    out_ref[rows, lanes] = jnp.zeros((CHANNELS, CHANNELS), jnp.bfloat16)


def front_kernel(blocks, edge_ref, x_hbm, left_ref, right_ref, *rest):
    top_ref = bottom_ref = None
    if blocks == OUTER:
        top_ref, bottom_ref = rest[:2]
        rest = rest[2:]
    weights_hbm, out_hbm = rest[:3], rest[3]
    stage, sides, xab, firsts, fab, seconds, out_ref, x_ref = rest[4:12]
    c1_ref, c2_ref, w1_ref, w2_ref, wm_ref, sems = rest[12:]
    lat, lon = edge_ref[0], edge_ref[1]
    keep = [
        jnp.where(inside, 1.0, 0.0)
        for inside in (lon > 0, lon < edge_ref[3] - 1, lat > 0, lat < edge_ref[2] - 1)
    ]
    spans = [
        [
            (max(start, 0), min(start + 20, ROWS), max(-start, 0))
            for start in (64 * p + 16 * block - 2 for p in range(2))
        ]
        for block in blocks
    ]
    fills = [
        [
            pltpu.make_async_copy(
                x_hbm.at[pl.ds(low, high - low)],
                x_ref.at[2 * at + p, pl.ds(0, high - low)],
                sems.at[2 + 2 * at + p],
            )
            for p, (low, high, _) in enumerate(pair)
        ]
        for at, pair in enumerate(spans)
    ]
    loads = [
        pltpu.make_async_copy(source, target, sems.at[6 + i])
        for i, (source, target) in enumerate(zip(weights_hbm, (c1_ref, c2_ref, wm_ref)))
    ]
    for copy in fills[0] + loads[:1] + fills[1] + loads[1:]:
        copy.start()
    stores = [
        pltpu.make_async_copy(
            out_ref.at[pl.ds(8 * i, 8)], out_hbm.at[pl.ds(8 * i, 8)], sems.at[i]
        )
        for i in range(2)
    ]
    pair_columns(None, w1_ref)
    pair_columns(None, w2_ref)
    sides[0:2] = left_ref[...].astype(jnp.float32)
    sides[2:4] = right_ref[...].astype(jnp.float32)
    sub = lax.broadcasted_iota(jnp.int32, (4 * MERGE, 8, LATENT), 1)
    for at, block in enumerate(blocks):
        for p in range(2):
            low, high, skip = spans[at][p]
            count = high - low
            fills[at][p].wait()

            def place(r, carry, at=at, p=p, skip=skip):
                to = pl.multiple_of((p * STAGE_ROWS + skip + r) * STRIDE + LEAD, 8)
                stage[pl.ds(to, COLS), :] = x_ref[2 * at + p, r].astype(jnp.float32)
                return carry

            lax.fori_loop(0, count, place, 0, unroll=2)
            base = (p * STAGE_ROWS + skip) * STRIDE
            for c in range(2):
                stage[pl.ds(base + LEAD - 2 + c, count, stride=STRIDE), :] = sides[c, low:high, :]
                stage[pl.ds(base + LEAD + COLS + c, count, stride=STRIDE), :] = sides[
                    2 + c, low:high, :
                ]
            for ends_ref, wanted, first in (
                (top_ref, skip > 0, 0),
                (bottom_ref, skip + count < 20, 18),
            ):
                if wanted:
                    tail = ends_ref[2 * COLS :, :].astype(jnp.float32)
                    for r in range(2):
                        to = (p * STAGE_ROWS + first + r) * STRIDE + LEAD
                        stage[to : to + COLS, :] = ends_ref[r * COLS : (r + 1) * COLS].astype(
                            jnp.float32
                        )
                        for c in range(2):
                            stage[to - 2 + c : to - 1 + c, :] = tail[2 * c + r : 2 * c + r + 1]
                            stage[to + COLS + c : to + COLS + c + 1, :] = tail[
                                4 + 2 * c + r : 5 + 2 * c + r
                            ]
        for p in range(2):
            for r in range(20):
                base = (p * STAGE_ROWS + r) * STRIDE + LEAD
                xab[p, r] = jnp.concatenate(
                    [stage[pl.ds(base + k, PAIRS, stride=2), :] for k in (-2, -1, 0, 1)], axis=-1
                ).astype(jnp.bfloat16)
        if at == 0:
            loads[0].wait()
            pair_columns(c1_ref, w1_ref)
        for p in range(2):
            for r0 in range(0, 18, CONV_ONE):
                lhs = jnp.concatenate([xab[p, r0 + dy : r0 + dy + CONV_ONE] for dy in range(3)], axis=-1)
                y = gelu(
                    jnp.dot(
                        lhs.reshape(CONV_ONE * PAIRS, 1536),
                        w1_ref[...],
                        preferred_element_type=jnp.float32,
                    )
                )
                for r in range(CONV_ONE):
                    to = (p * FIRST_ROWS + r0 + r) * FIRST_STRIDE
                    for m in range(2):
                        firsts[m, to : to + PAIRS, :] = y[
                            r * PAIRS : (r + 1) * PAIRS, m * CHANNELS : (m + 1) * CHANNELS
                        ]
        lhs = jnp.concatenate(
            [
                jnp.concatenate(
                    [
                        stage[
                            pl.ds(
                                (p * STAGE_ROWS + dy) * STRIDE + LEAD + COLS - 2 + k,
                                FIRST_ROWS,
                                stride=STRIDE,
                            ),
                            :,
                        ]
                        for dy in range(3)
                        for k in range(4)
                    ],
                    axis=-1,
                )
                for p in range(2)
            ],
            axis=0,
        ).astype(jnp.bfloat16)
        edge = gelu(jnp.dot(lhs, w1_ref[...], preferred_element_type=jnp.float32))
        for p in range(2):
            base = p * FIRST_ROWS * FIRST_STRIDE
            mine = edge[p * FIRST_ROWS : (p + 1) * FIRST_ROWS]
            last = pl.ds(base + PAIRS, FIRST_ROWS, stride=FIRST_STRIDE)
            firsts[0, last, :] = mine[:, 0:CHANNELS]
            firsts[1, last, :] = mine[:, CHANNELS:] * keep[1]
            begin = pl.ds(base, FIRST_ROWS, stride=FIRST_STRIDE)
            firsts[0, begin, :] = firsts[0, begin, :] * keep[0]
        if block == 0:
            firsts[:, 0:FIRST_STRIDE, :] = firsts[:, 0:FIRST_STRIDE, :] * keep[2]
        if block == 3:
            to = (FIRST_ROWS + 17) * FIRST_STRIDE
            firsts[:, to : to + FIRST_STRIDE, :] = firsts[:, to : to + FIRST_STRIDE, :] * keep[3]
        for p in range(2):
            for r in range(18):
                base = (p * FIRST_ROWS + r) * FIRST_STRIDE
                fab[p, r] = jnp.concatenate(
                    [firsts[m, base + k : base + k + PAIRS, :] for k in range(2) for m in range(2)],
                    axis=-1,
                ).astype(jnp.bfloat16)
        if at == 0:
            loads[1].wait()
            loads[2].wait()
            pair_columns(c2_ref, w2_ref)
        for p in range(2):
            for r0 in range(0, 16, CONV_TWO):
                lhs = jnp.concatenate(
                    [fab[p, r0 + dy : r0 + dy + CONV_TWO] for dy in range(3)], axis=-1
                )
                s = gelu(
                    jnp.dot(
                        lhs.reshape(CONV_TWO * PAIRS, 1536),
                        w2_ref[...],
                        preferred_element_type=jnp.float32,
                    )
                ).astype(jnp.bfloat16)
                s = s.reshape(CONV_TWO // 2, 2, PAIRS, 256)
                to = slice(r0 // 2, (r0 + CONV_TWO) // 2)
                seconds[p, to, :, 0:256] = s[:, 0]
                seconds[p, to, :, 256:512] = s[:, 1]
        for r0 in range(0, 8, MERGE):
            zero, one = [
                jnp.dot(
                    seconds[p, r0 : r0 + MERGE].reshape(MERGE * PAIRS, LATENT),
                    wm_ref[...],
                    preferred_element_type=jnp.float32,
                ).reshape(MERGE * 4, 8, LATENT)
                for p in range(2)
            ]
            even = jnp.where(sub < 4, zero, pltpu.roll(one, 4, 1))
            odd = jnp.where(sub < 4, pltpu.roll(zero, 4, 1), one)
            to = slice(8 * at + r0, 8 * at + r0 + MERGE)
            out_ref[to, :, 0] = even.reshape(MERGE, 4, 8, LATENT).astype(jnp.bfloat16)
            out_ref[to, :, 1] = odd.reshape(MERGE, 4, 8, LATENT).astype(jnp.bfloat16)
        stores[at].start()
    for store in stores:
        store.wait()


def front(blocks, place, x, left, right, ends, c1, c2, wm):
    vmem = pl.BlockSpec(memory_space=pltpu.VMEM)
    hbm = pl.BlockSpec(memory_space=pltpu.HBM)
    args = (x, left, right) + tuple(ends) + (c1, c2, wm)
    out = pl.pallas_call(
        functools.partial(front_kernel, blocks),
        out_shape=jax.ShapeDtypeStruct((16, 4, 2, 8, LATENT), jnp.bfloat16),
        in_specs=[pl.BlockSpec(memory_space=pltpu.SMEM), hbm]
        + [vmem] * (2 + len(ends))
        + [hbm] * 3,
        out_specs=hbm,
        scratch_shapes=[
            pltpu.VMEM((2 * STAGE_ROWS * STRIDE, CHANNELS), jnp.float32),
            pltpu.VMEM((4, ROWS, CHANNELS), jnp.float32),
            pltpu.VMEM((2, 20, PAIRS, 512), jnp.bfloat16),
            pltpu.VMEM((2, 2 * FIRST_ROWS * FIRST_STRIDE, CHANNELS), jnp.float32),
            pltpu.VMEM((2, 18, PAIRS, 512), jnp.bfloat16),
            pltpu.VMEM((2, 8, PAIRS, LATENT), jnp.bfloat16),
            pltpu.VMEM((16, 4, 2, 8, LATENT), jnp.bfloat16),
            pltpu.VMEM((4, 20, COLS, CHANNELS), jnp.bfloat16),
            pltpu.VMEM((3, 3, CHANNELS, CHANNELS), jnp.bfloat16),
            pltpu.VMEM((3, 3, CHANNELS, CHANNELS), jnp.bfloat16),
            pltpu.VMEM((1536, 256), jnp.bfloat16),
            pltpu.VMEM((1536, 256), jnp.bfloat16),
            pltpu.VMEM((LATENT, LATENT), jnp.bfloat16),
            pltpu.SemaphoreType.DMA((9,)),
        ],
        compiler_params=pltpu.CompilerParams(vmem_limit_bytes=LIMIT),
        cost_estimate=pl.CostEstimate(
            flops=8_000_000_000, transcendentals=1_100_000, bytes_accessed=5_000_000
        ),
        name="front_inner" if blocks == INNER else "front_outer",
    )(place, *args)
    return out.reshape(128, 8, LATENT)


def layer_norm(v, gain):
    center = v - jnp.mean(v, axis=-1, keepdims=True)
    spread = jnp.mean(center * center, axis=-1, keepdims=True)
    return center * lax.rsqrt(spread + EPSILON) * gain


def middle_kernel(
    tok_hbm,
    gains_ref,
    qgain_ref,
    win_hbm,
    wout_hbm,
    wi_hbm,
    wd_hbm,
    out_hbm,
    cells,
    staged,
    win_ref,
    wout_ref,
    wi_ref,
    wd_ref,
    sems,
):
    sources = (wout_hbm, wi_hbm, wd_hbm)
    targets = (wout_ref, wi_ref, wd_ref)
    loads = [
        pltpu.make_async_copy(source, target, sems.at[i])
        for i, (source, target) in enumerate(zip(sources, targets))
    ]
    fills = [
        pltpu.make_async_copy(
            tok_hbm.at[pl.ds(32 * i, 32)], staged.at[pl.ds(32 * i, 32)], sems.at[3 + i]
        )
        for i in range(4)
    ]
    parts = [
        pltpu.make_async_copy(
            win_hbm.at[pl.ds(LATENT * i, LATENT)], win_ref.at[pl.ds(LATENT * i, LATENT)], sems.at[7 + i]
        )
        for i in range(3)
    ]
    for load in fills + parts + loads:
        load.start()
    for i, fill in enumerate(fills):
        fill.wait()
        held = staged[32 * i : 32 * (i + 1)].reshape(256, LATENT).astype(jnp.float32)
        for q in range(4):
            cells[q, 256 * i : 256 * (i + 1)] = held[:, q * 128 : (q + 1) * 128]
    for part in parts:
        part.wait()

    def window(step, carry):
        places = [pl.ds(step + WINDOWS * p, 128, stride=8) for p in range(2)]
        tokens = jnp.concatenate(
            [jnp.concatenate([cells[q, place, :] for q in range(4)], axis=-1) for place in places],
            axis=0,
        )
        normed = layer_norm(tokens, gains_ref[0:1, :]).astype(jnp.bfloat16)
        projected = lax.dot_general(
            win_ref[...], normed, (((1,), (1,)), ((), ())), preferred_element_type=jnp.float32
        )

        def scaled(part):
            heads = part.reshape(NUM_HEADS, HEAD_WIDTH, 256)
            square = jnp.mean(heads * heads, axis=1, keepdims=True)
            return (heads * lax.rsqrt(jnp.maximum(square, FLOOR))).reshape(LATENT, 256)

        qgain = jnp.concatenate([qgain_ref[...], qgain_ref[...]], axis=-1)
        queries = (scaled(projected[0:LATENT]) * qgain).astype(jnp.bfloat16)
        keys = scaled(projected[LATENT : 2 * LATENT]).T.astype(jnp.bfloat16)
        values = projected[2 * LATENT :].astype(jnp.bfloat16)
        blank = jnp.zeros((HEAD_WIDTH, 256), jnp.bfloat16)
        row = lax.broadcasted_iota(jnp.int32, (16, 256), 0)
        marks = [jnp.where(row == i, 1.0, 0.0).astype(jnp.bfloat16) for i in range(GROUP)]
        attended = []
        for group in range(NUM_HEADS // GROUP):
            heads = [
                slice((GROUP * group + i) * HEAD_WIDTH, (GROUP * group + i + 1) * HEAD_WIDTH)
                for i in range(GROUP)
            ]
            right = jnp.concatenate(
                [
                    jnp.concatenate([queries[heads[i]] if k == i else blank for k in range(GROUP)], axis=0)
                    for i in range(GROUP)
                ],
                axis=1,
            )
            scores = jnp.dot(
                keys[:, group * GROUP * 32 : (group + 1) * GROUP * 32], right, preferred_element_type=jnp.float32
            )
            expon = jnp.exp2(scores).astype(jnp.bfloat16)
            left = jnp.concatenate(
                [
                    jnp.concatenate(
                        [values[heads[i]] if k == i else blank for k in range(GROUP)] + [marks[i]],
                        axis=0,
                    )
                    for i in range(GROUP)
                ],
                axis=1,
            )
            stacked = jnp.concatenate([expon[:, 256 * i : 256 * (i + 1)] for i in range(GROUP)], axis=0)
            both = jnp.dot(left, stacked, preferred_element_type=jnp.float32)
            inverse = 1.0 / both[32 * GROUP : 32 * GROUP + 8]
            for i in range(GROUP):
                attended.append(both[32 * i : 32 * (i + 1)] * inverse[i : i + 1])
        attended = jnp.concatenate(attended, axis=0).T.astype(jnp.bfloat16)

        @pl.when(step == 0)
        def _():
            loads[0].wait()

        mixed = tokens + jnp.dot(attended, wout_ref[...], preferred_element_type=jnp.float32)
        for p in range(2):
            for q in range(4):
                cells[q, places[p], :] = mixed[128 * p : 128 * (p + 1), 128 * q : 128 * (q + 1)]
        return carry

    lax.fori_loop(0, WINDOWS, window, 0, unroll=2)
    loads[1].wait()
    loads[2].wait()
    stores = []
    for at in range(1024 // MLP_ROWS):
        place = slice(at * MLP_ROWS, (at + 1) * MLP_ROWS)
        mixed = jnp.concatenate([cells[q, place, :] for q in range(4)], axis=-1)
        mixed = mixed.astype(jnp.bfloat16).astype(jnp.float32)
        normed_two = layer_norm(mixed, gains_ref[3:4, :]).astype(jnp.bfloat16)
        updated = mixed
        for j in range(MLP_WIDTH // MLP_PART):
            part = slice(j * MLP_PART, (j + 1) * MLP_PART)
            inner = gelu(
                jnp.dot(normed_two, wi_ref[:, part], preferred_element_type=jnp.float32)
            ).astype(jnp.bfloat16)
            updated = updated + jnp.dot(inner, wd_ref[part, :], preferred_element_type=jnp.float32)
        blocks = pl.ds(at * (MLP_ROWS // 8), MLP_ROWS // 8)
        staged[blocks] = updated.astype(jnp.bfloat16).reshape(MLP_ROWS // 8, 8, LATENT)
        store = pltpu.make_async_copy(staged.at[blocks], out_hbm.at[blocks], sems.at[10 + at])
        store.start()
        stores.append(store)
    for store in stores:
        store.wait()


def middle(tokens, gains, qgain, win, wout, wi, wd):
    vmem = pl.BlockSpec(memory_space=pltpu.VMEM)
    hbm = pl.BlockSpec(memory_space=pltpu.HBM)
    return pl.pallas_call(
        middle_kernel,
        out_shape=jax.ShapeDtypeStruct((128, 8, LATENT), jnp.bfloat16),
        in_specs=[hbm] + [vmem] * 2 + [hbm] * 4,
        out_specs=hbm,
        scratch_shapes=[
            pltpu.VMEM((4, 1024, 128), jnp.float32),
            pltpu.VMEM((128, 8, LATENT), jnp.bfloat16),
            pltpu.VMEM((3 * LATENT, LATENT), jnp.bfloat16),
            pltpu.VMEM((LATENT, LATENT), jnp.bfloat16),
            pltpu.VMEM((LATENT, MLP_WIDTH), jnp.bfloat16),
            pltpu.VMEM((MLP_WIDTH, LATENT), jnp.bfloat16),
            pltpu.SemaphoreType.DMA((10 + 1024 // MLP_ROWS,)),
        ],
        compiler_params=pltpu.CompilerParams(vmem_limit_bytes=LIMIT),
        cost_estimate=pl.CostEstimate(
            flops=16_000_000_000, transcendentals=6_000_000, bytes_accessed=9_000_000
        ),
        name="middle",
    )(tokens, gains, qgain, win, wout, wi, wd)


def back_kernel(cells_ref, x_ref, we_ref, *rest):
    out_ref, even, odd = rest[-3:]
    expanded = jnp.dot(
        cells_ref[...].reshape(512, LATENT), we_ref[...], preferred_element_type=jnp.float32
    )
    for di, held in enumerate((even, odd)):
        for dj in range(2):
            lanes = (2 * di + dj) * CHANNELS
            held[pl.ds(dj, 512, stride=2), :] = expanded[:, lanes : lanes + CHANNELS]
    for di, held in enumerate((even, odd)):
        for u in range(8):
            rows = held[u * 128 : (u + 1) * 128, :].reshape(8, 2, 8, CHANNELS)
            for p in range(2):
                fine = rows[:, p].reshape(COLS, CHANNELS)
                old = x_ref[p, 2 * u + di].astype(jnp.float32)
                out_ref[p, 2 * u + di] = (fine + old).astype(jnp.bfloat16)


def back(blocks, cells, x, we, before):
    step = blocks[1] - blocks[0]
    fine = pl.BlockSpec((2, 16, COLS, CHANNELS), lambda i: (0, blocks[0] + step * i, 0, 0))
    specs = [
        pl.BlockSpec((64, 8, LATENT), lambda i: (i, 0, 0)),
        fine,
        pl.BlockSpec((LATENT, LATENT), lambda i: (0, 0), pipeline_mode=pl.Buffered(1)),
    ]
    args = (cells, x, we)
    aliases = {}
    if before is not None:
        specs.append(pl.BlockSpec(memory_space=pl.ANY))
        args += (before,)
        aliases = {3: 0}
    return pl.pallas_call(
        back_kernel,
        out_shape=jax.ShapeDtypeStruct((2, 64, COLS, CHANNELS), jnp.bfloat16),
        grid=(2,),
        in_specs=specs,
        out_specs=fine,
        scratch_shapes=[pltpu.VMEM((1024, CHANNELS), jnp.float32)] * 2,
        input_output_aliases=aliases,
        compiler_params=pltpu.CompilerParams(vmem_limit_bytes=16 << 20),
        cost_estimate=pl.CostEstimate(
            flops=540_000_000, transcendentals=0, bytes_accessed=4_000_000
        ),
        name="back_inner" if blocks == INNER else "back_outer",
    )(*args)


def from_before(cells, axis):
    ends = lax.axis_size(axis) - 1
    return lax.ppermute(cells, axis, [(i, i + 1) for i in range(ends)])


def from_after(cells, axis):
    ends = lax.axis_size(axis) - 1
    return lax.ppermute(cells, axis, [(i + 1, i) for i in range(ends)])


def per_device(
    x,
    conv_one,
    conv_two,
    merge_weight,
    norm_gains,
    attention_in,
    attention_out,
    dense_in,
    dense_out,
    expand_weight,
):
    place = jnp.stack(
        [
            jnp.int32(at)
            for at in (
                lax.axis_index("lat"),
                lax.axis_index("lon"),
                lax.axis_size("lat"),
                lax.axis_size("lon"),
            )
        ]
    )
    left = from_before(x[:, COLS - 2 :, :].transpose(1, 0, 2), "lon")
    right = from_after(x[:, :2, :].transpose(1, 0, 2), "lon")
    win = attention_in.T
    scale = HEAD_WIDTH**-0.5 * math.log2(math.e)
    qgain = jnp.broadcast_to(
        (norm_gains[1] * norm_gains[2] * scale)[:, None], (LATENT, 128)
    )

    def wide(rows):
        return jnp.concatenate(
            [
                x[rows].reshape(2 * COLS, CHANNELS),
                left[:, rows].reshape(4, CHANNELS),
                right[:, rows].reshape(4, CHANNELS),
            ],
            axis=0,
        )

    top = from_before(wide(slice(ROWS - 2, ROWS)), "lat")
    bottom = from_after(wide(slice(0, 2)), "lat")
    exchange = functools.partial(
        lax.all_to_all, axis_name=("lat", "lon"), split_axis=0, concat_axis=0, tiled=True
    )
    inner = front(INNER, place, x, left, right, (), conv_one, conv_two, merge_weight)
    inner, top, bottom, win = lax.optimization_barrier((inner, top, bottom, win))
    inner = exchange(inner)
    outer = front(OUTER, place, x, left, right, (top, bottom), conv_one, conv_two, merge_weight)
    outer = exchange(outer)
    weights = (norm_gains, qgain, win, attention_out, dense_in, dense_out)
    inner = exchange(middle(inner, *weights))
    outer = exchange(middle(outer, *weights))
    field = x.reshape(2, 64, COLS, CHANNELS)
    result = back(INNER, inner, field, expand_weight, None)
    result = back(OUTER, outer, field, expand_weight, result)
    return result.reshape(ROWS, COLS, CHANNELS)


def solution(mesh):
    return jax.shard_map(
        per_device,
        mesh=mesh,
        in_specs=(P("lat", "lon", None), P(), P(), P(), P(), P(), P(), P(), P(), P()),
        out_specs=P("lat", "lon", None),
        check_vma=False,
    )
```

time: 183 us -> 148 us (0.81)
  local copies, waits for them, and re-layouts: 27.7 us -> 9.7 us
  Pallas kernels: 76.7 us -> 63.4 us
  starting transfers between devices: 52.8 us -> 47.7 us
  waiting for transfers between devices: 21.7 us -> 25.7 us
  other arithmetic: 2.66 us -> 0.7 us
    unnamed x51 -> x27, local copies, waits for them, and re-layouts: 25.4 us -> 6.91 us
    pallas_call x2, Pallas kernels: 54.7 us -> 41.5 us  [middle(): pl.pallas_call(middle_kernel, out_shape=jax.ShapeDtypeStruct((128, 8, LAT...]
    all_to_all x1, waiting for transfers between devices: 0.01 us -> 9.78 us  [per_device(): inner = exchange(inner)]
    ppermute x2, waiting for transfers between devices: 6.98 us -> 1.11 us  [from_after(): return lax.ppermute(cells, axis, [(i + 1, i) for i in range(ends)])]
    all_to_all x1, starting transfers between devices: 10.6 us -> 4.84 us  [per_device(): outer = exchange(outer)]
    concatenate x2, other arithmetic: 2.57 us -> 0.02 us  [wide(): jnp.concatenate([x[rows].reshape(2 * COLS, CHANNELS), left[:, rows].resha...]
  transfers between devices with their start and end apart: 8 -> 8, of which waited for: 3 -> 3; matrix products, arithmetic and copies ran while one was open for 3% -> 3% of each run, Pallas kernels for 36% -> 42%
where the time goes in v1:
time: 148 us; the launch traced here: 147 us
  Pallas kernels  63.4 us (43%)
  starting transfers between devices  47.7 us (32%)
  waiting for transfers between devices  25.7 us (17%)
  local copies, waits for them, and re-layouts  9.7 us (7%)
    pallas_call x2, Pallas kernels, middle(): pl.pallas_call(middle_kernel, out_shape=jax.ShapeDtypeStruct((128, 8, LAT...  41.5 us
    pallas_call x2, Pallas kernels, front(): pl.pallas_call(functools.partial(front_kernel, blocks), out_shape=jax.Sha...  18.2 us
    all_to_all x1, waiting for transfers between devices, per_device(): outer = exchange(middle(outer, *weights))  14.7 us
    all_to_all x1, starting transfers between devices, per_device(): inner = exchange(inner)  10.1 us
    ppermute x2, starting transfers between devices, from_before(): return lax.ppermute(cells, axis, [(i, i + 1) for i in range(ends)])  10 us
    all_to_all x1, waiting for transfers between devices, per_device(): inner = exchange(inner)  9.78 us
    all_to_all x1, starting transfers between devices, per_device(): inner = exchange(middle(inner, *weights))  9.78 us
    all_to_all x1, starting transfers between devices, per_device(): outer = exchange(middle(outer, *weights))  9.76 us
  transfers between devices with their start and end apart: 8, of which 3 were waited for; matrix products, arithmetic and copies ran while one was open for 3% of the time, Pallas kernels for 42%

profile of v1, /device:TPU:1, one launch (start us, length us, event | category | flops | bytes accessed | tf_op | source)
XLA Modules:
  0.0 147.5 jit_solution(2661216043436391495)
XLA Ops:
  0.0 1.1 fusion.1
  1.2 6.9 %collective-permute-start = (bf16[2,128,128]{2,1,0:T(8,128)(2,1)S(1)}, bf16[2,128,128]{2,1,0:T(8,128)(2,1)S(1)}, u32[]{:S(2)}, u32[]{:S(2)}) collective-permute-start(bf16[2,128,128]{2,1,0:T(8,128)(2,1)S(1)} %bitcast.28), channel_id=1, source_target_pairs={{0,1},{1,2},{2,3},{3,4},{4,5},{5,6},{6,7},{7,8},{8,9},{9,10},{10,1... | collective-permute-start | bytes 196616 | tf_op jit(solution)/shard_map/ppermute | solution.py:499
  8.1 1.9 %collective-permute-start.1 = (bf16[2,128,128]{2,1,0:T(8,128)(2,1)S(1)}, bf16[2,128,128]{2,1,0:T(8,128)(2,1)S(1)}, u32[]{:S(2)}, u32[]{:S(2)}) collective-permute-start(bf16[2,128,128]{2,1,0:T(8,128)(2,1)S(1)} %bitcast.29), channel_id=1, source_target_pairs={{1,0},{2,1},{3,2},{4,3},{5,4},{6,5},{7,6},{8,7},{9,8},{10,9},{11,1... | collective-permute-start | bytes 196616 | tf_op jit(solution)/shard_map/ppermute | solution.py:504
  10.0 0.8 fusion
  10.8 2.6 %copy.14 = bf16[512,1536]{0,1:T(8,128)(2,1)} copy(bf16[512,1536]{1,0:T(8,128)(2,1)} %param.15) | data formatting | bytes 3145728 | tf_op args[5]
  13.4 0.7 pad_add_fusion.edge_ref
  14.1 0.0 collective-permute-done.left_ref
  14.1 0.0 copy-start.8
  14.1 1.1 collective-permute-done.1.right_ref
  15.2 0.0 copy-start.9
  15.2 3.1 %collective-permute-start.2 = (bf16[136,128]{1,0:T(8,128)(2,1)S(1)}, bf16[136,128]{1,0:T(8,128)(2,1)S(1)}, u32[]{:S(2)}, u32[]{:S(2)}) collective-permute-start(bf16[136,128]{1,0:T(8,128)(2,1)S(1)} %pad_maximum_fusion), channel_id=1, source_target_pairs={{0,16},{16,32},{32,48},{48,64},{64,80},{80,96},{96,112},{1,17},{17... | collective-permute-start | bytes 104456 | tf_op jit(solution)/shard_map/ppermute | solution.py:499
  18.3 1.3 collective-permute-start.3
  19.6 0.0 copy-done.8
  19.7 0.0 copy-done.9
  19.7 9.1 %front_inner.1 = bf16[16,4,2,8,512]{4,3,2,1,0:T(8,128)(2,1)} custom-call(s32[4]{0:T(128)} %pad_add_fusion.edge_ref, bf16[128,64,128]{2,1,0:T(8,128)(2,1)} %x_hbm.3, bf16[2,128,128]{2,1,0:T(8,128)(2,1)} %copy-done.8, bf16[2,128,128]{2,1,0:T(8,128)(2,1)} %copy-done.9, bf16[3,3,128,128]{3,2,1,0:T(8,128)(2,1)} %rest_2_.3, bf16[3,3,128,128]{3,2,1,0:T(8,128)(2,1)} %rest_3_.1, ...), custom_call_target="tpu_custom_call" | custom-call | flops 8000000000 | bytes 5000000 | tf_op jit(solution)/shard_map/front_inner/pallas_call | solution.py:249
  28.8 0.0 copy-start.7
  28.8 0.0 collective-permute-done.2.rest_0_
  28.8 0.0 copy-start.10
  28.8 0.0 collective-permute-done.3.rest_1_
  28.8 0.0 copy-start.11
  28.8 10.1 %all-to-all-start.2 = ((bf16[128,8,512]{2,1,0:T(8,128)(2,1)}), bf16[128,8,512]{2,1,0:T(8,128)(2,1)S(1)}, u32[]{:S(2)}, u32[]{:S(2)}) async-start(bf16[128,8,512]{2,1,0:T(8,128)(2,1)} %bitcast.24), calls=%async_computation.2 | async-start | bytes 2097152 | tf_op jit(solution)/shard_map/all_to_all | solution.py:555
  38.9 0.0 copy-done.7
  38.9 0.0 copy-done.10
  39.0 0.0 copy-done.11
  39.0 9.1 %front_outer.1 = bf16[16,4,2,8,512]{4,3,2,1,0:T(8,128)(2,1)} custom-call(s32[4]{0:T(128)} %pad_add_fusion.edge_ref, bf16[128,64,128]{2,1,0:T(8,128)(2,1)} %x_hbm.3, bf16[2,128,128]{2,1,0:T(8,128)(2,1)} %copy-done.8, bf16[2,128,128]{2,1,0:T(8,128)(2,1)} %copy-done.9, bf16[136,128]{1,0:T(8,128)(2,1)} %copy-done.10, bf16[136,128]{1,0:T(8,128)(2,1)} %copy-done.11, ...), custom_call_target="tpu_custom_call" | custom-call | flops 8000000000 | bytes 5000000 | tf_op jit(solution)/shard_map/front_outer/pallas_call | solution.py:249
  48.1 9.8 %all-to-all-done.2.tok_hbm = bf16[128,8,512]{2,1,0:T(8,128)(2,1)S(1)} async-done(((bf16[128,8,512]{2,1,0:T(8,128)(2,1)}), bf16[128,8,512]{2,1,0:T(8,128)(2,1)S(1)}, u32[]{:S(2)}, u32[]{:S(2)}) %all-to-all-start.2) | async-done | bytes 1048608 | tf_op jit(solution)/shard_map/all_to_all | solution.py:555
  57.8 0.0 copy-start.5
  57.8 4.8 %all-to-all-start = ((bf16[128,8,512]{2,1,0:T(8,128)(2,1)}), bf16[128,8,512]{2,1,0:T(8,128)(2,1)S(1)}, u32[]{:S(2)}, u32[]{:S(2)}) async-start(bf16[128,8,512]{2,1,0:T(8,128)(2,1)} %bitcast.25), calls=%async_computation | async-start | bytes 2097152 | tf_op jit(solution)/shard_map/all_to_all | solution.py:557
  62.7 0.9 broadcast_in_dim.2.qgain_ref
  63.6 0.0 copy-done.5
  63.6 20.7 %middle.3 = bf16[128,8,512]{2,1,0:T(8,128)(2,1)} custom-call(bf16[128,8,512]{2,1,0:T(8,128)(2,1)} %copy-done.5, f32[4,512]{1,0:T(4,128)} %gains_ref.3, f32[512,128]{1,0:T(8,128)} %broadcast_in_dim.2.qgain_ref, bf16[1536,512]{1,0:T(8,128)(2,1)} %bitcast.22, bf16[512,512]{1,0:T(8,128)(2,1)} %wout_hbm.3, bf16[512,2048]{1,0:T(8,128)(2,1)} %wi_hbm.3, ...), custom_call_target="tpu_custom_call" | custom-call | flops 16000000000 | bytes 9000000 | tf_op jit(solution)/shard_map/middle/pallas_call | solution.py:427
  84.3 0.0 all-to-all-done.tok_hbm
  84.3 0.0 copy-start.6
  84.3 9.8 %all-to-all-start.3 = ((bf16[128,8,512]{2,1,0:T(8,128)(2,1)}), bf16[128,8,512]{2,1,0:T(8,128)(2,1)S(1)}, u32[]{:S(2)}, u32[]{:S(2)}) async-start(bf16[128,8,512]{2,1,0:T(8,128)(2,1)} %middle.3), calls=%async_computation.3 | async-start | bytes 2097152 | tf_op jit(solution)/shard_map/all_to_all | solution.py:559
  94.1 0.0 copy-done.6
  94.1 20.7 %middle.2 = bf16[128,8,512]{2,1,0:T(8,128)(2,1)} custom-call(bf16[128,8,512]{2,1,0:T(8,128)(2,1)} %copy-done.6, f32[4,512]{1,0:T(4,128)} %gains_ref.3, f32[512,128]{1,0:T(8,128)} %broadcast_in_dim.2.qgain_ref, bf16[1536,512]{1,0:T(8,128)(2,1)} %bitcast.23, bf16[512,512]{1,0:T(8,128)(2,1)} %wout_hbm.3, bf16[512,2048]{1,0:T(8,128)(2,1)} %wi_hbm.3, ...), custom_call_target="tpu_custom_call" | custom-call | flops 16000000000 | bytes 9000000 | tf_op jit(solution)/shard_map/middle/pallas_call | solution.py:427
  114.9 0.0 copy-start
  114.9 0.0 all-to-all-done.3.cells_ref
  114.9 0.0 copy-start.1
  114.9 1.0 copy-done.1
  115.8 9.8 %all-to-all-start.1 = ((bf16[128,8,512]{2,1,0:T(8,128)(2,1)}), bf16[128,8,512]{2,1,0:T(8,128)(2,1)S(1)}, u32[]{:S(2)}, u32[]{:S(2)}) async-start(bf16[128,8,512]{2,1,0:T(8,128)(2,1)} %middle.2), calls=%async_computation.1 | async-start | bytes 2097152 | tf_op jit(solution)/shard_map/all_to_all | solution.py:560
  125.6 0.0 copy-done
  125.6 0.0 copy-start.2
  125.6 1.2 copy-done.2
  126.9 0.0 copy-start.3
  126.9 1.0 copy-done.3
  127.9 1.9 %back_inner.1.rest_0_ = bf16[2,64,64,128]{3,2,1,0:T(8,128)(2,1)} custom-call(bf16[128,8,512]{2,1,0:T(8,128)(2,1)S(1)} %copy-done.2, bf16[2,64,64,128]{3,2,1,0:T(8,128)(2,1)S(1)} %bitcast.20, bf16[512,512]{1,0:T(8,128)(2,1)S(1)} %copy-done.3), custom_call_target="tpu_custom_call" | custom-call | flops 540000000 | bytes 4000000 | tf_op jit(solution)/shard_map/back_inner/pallas_call | solution.py:481
  129.8 14.7 %all-to-all-done.1.cells_ref = bf16[128,8,512]{2,1,0:T(8,128)(2,1)S(1)} async-done(((bf16[128,8,512]{2,1,0:T(8,128)(2,1)}), bf16[128,8,512]{2,1,0:T(8,128)(2,1)S(1)}, u32[]{:S(2)}, u32[]{:S(2)}) %all-to-all-start.1) | async-done | bytes 1048608 | tf_op jit(solution)/shard_map/all_to_all | solution.py:560
  144.5 0.0 copy-start.4
  144.5 1.0 copy-done.4
  145.6 1.9 %back_outer.1 = bf16[2,64,64,128]{3,2,1,0:T(8,128)(2,1)} custom-call(bf16[128,8,512]{2,1,0:T(8,128)(2,1)S(1)} %all-to-all-done.1.cells_ref, bf16[2,64,64,128]{3,2,1,0:T(8,128)(2,1)S(1)} %bitcast.21, bf16[512,512]{1,0:T(8,128)(2,1)S(1)} %copy-done.4, bf16[2,64,64,128]{3,2,1,0:T(8,128)(2,1)} %back_inner.1.rest_0_), custom_call_target="tpu_custom_call", output_to_operand_aliasing={{}: (3, {})} | custom-call | flops 540000000 | bytes 4000000 | tf_op jit(solution)/shard_map/back_outer/pallas_call | solution.py:481
  (7 shorter events, 0.1 us)
Async XLA Ops:
  1.2 12.9 %collective-permute-start = (bf16[2,128,128]{2,1,0:T(8,128)(2,1)S(1)}, bf16[2,128,128]{2,1,0:T(8,128)(2,1)S(1)}, u32[]{:S(2)}, u32[]{:S(2)}) collective-permute-start(bf16[2,128,128]{2,1,0:T(8,128)(2,1)S(1)} %bitcast.28), channel_id=1, source_target_pairs={{0,1},{1,2},{2,3},{3,4},{4,5},{5,6},{6,7},{7,8},{8,9},{9,10},{10,1... | collective-permute-start | bytes 196616 | tf_op jit(solution)/shard_map/ppermute | solution.py:499
  8.1 7.1 %collective-permute-start.1 = (bf16[2,128,128]{2,1,0:T(8,128)(2,1)S(1)}, bf16[2,128,128]{2,1,0:T(8,128)(2,1)S(1)}, u32[]{:S(2)}, u32[]{:S(2)}) collective-permute-start(bf16[2,128,128]{2,1,0:T(8,128)(2,1)S(1)} %bitcast.29), channel_id=1, source_target_pairs={{1,0},{2,1},{3,2},{4,3},{5,4},{6,5},{7,6},{8,7},{9,8},{10,9},{11,1... | collective-permute-start | bytes 196616 | tf_op jit(solution)/shard_map/ppermute | solution.py:504
  14.1 5.6 %copy-start.8 = (bf16[2,128,128]{2,1,0:T(8,128)(2,1)}, bf16[2,128,128]{2,1,0:T(8,128)(2,1)S(1)}, u32[]{:S(2)}) copy-start(bf16[2,128,128]{2,1,0:T(8,128)(2,1)S(1)} %collective-permute-done.left_ref) | copy-start | bytes 196612
  15.2 4.5 %copy-start.9 = (bf16[2,128,128]{2,1,0:T(8,128)(2,1)}, bf16[2,128,128]{2,1,0:T(8,128)(2,1)S(1)}, u32[]{:S(2)}) copy-start(bf16[2,128,128]{2,1,0:T(8,128)(2,1)S(1)} %collective-permute-done.1.right_ref) | copy-start | bytes 196612
  15.2 13.6 %collective-permute-start.2 = (bf16[136,128]{1,0:T(8,128)(2,1)S(1)}, bf16[136,128]{1,0:T(8,128)(2,1)S(1)}, u32[]{:S(2)}, u32[]{:S(2)}) collective-permute-start(bf16[136,128]{1,0:T(8,128)(2,1)S(1)} %pad_maximum_fusion), channel_id=1, source_target_pairs={{0,16},{16,32},{32,48},{48,64},{64,80},{80,96},{96,112},{1,17},{17... | collective-permute-start | bytes 104456 | tf_op jit(solution)/shard_map/ppermute | solution.py:499
  18.3 10.5 %collective-permute-start.3 = (bf16[136,128]{1,0:T(8,128)(2,1)S(1)}, bf16[136,128]{1,0:T(8,128)(2,1)S(1)}, u32[]{:S(2)}, u32[]{:S(2)}) collective-permute-start(bf16[136,128]{1,0:T(8,128)(2,1)S(1)} %pad_maximum_fusion.1), channel_id=1, source_target_pairs={{16,0},{32,16},{48,32},{64,48},{80,64},{96,80},{112,96},{17,1},{33... | collective-permute-start | bytes 104456 | tf_op jit(solution)/shard_map/ppermute | solution.py:504
  28.8 10.2 %copy-start.7 = (f32[4,512]{1,0:T(4,128)S(1)}, f32[4,512]{1,0:T(4,128)}, u32[]{:S(2)}) copy-start(f32[4,512]{1,0:T(4,128)} %gains_ref.3) | copy-start | bytes 24580
  28.8 10.2 %copy-start.10 = (bf16[136,128]{1,0:T(8,128)(2,1)}, bf16[136,128]{1,0:T(8,128)(2,1)S(1)}, u32[]{:S(2)}) copy-start(bf16[136,128]{1,0:T(8,128)(2,1)S(1)} %collective-permute-done.2.rest_0_) | copy-start | bytes 104452
  28.8 10.1 %copy-start.11 = (bf16[136,128]{1,0:T(8,128)(2,1)}, bf16[136,128]{1,0:T(8,128)(2,1)S(1)}, u32[]{:S(2)}) copy-start(bf16[136,128]{1,0:T(8,128)(2,1)S(1)} %collective-permute-done.3.rest_1_) | copy-start | bytes 104452
  28.8 29.0 %all-to-all-start.2 = ((bf16[128,8,512]{2,1,0:T(8,128)(2,1)}), bf16[128,8,512]{2,1,0:T(8,128)(2,1)S(1)}, u32[]{:S(2)}, u32[]{:S(2)}) async-start(bf16[128,8,512]{2,1,0:T(8,128)(2,1)} %bitcast.24), calls=%async_computation.2 | async-start | bytes 2097152 | tf_op jit(solution)/shard_map/all_to_all | solution.py:555
  57.8 5.7 %copy-start.5 = (bf16[128,8,512]{2,1,0:T(8,128)(2,1)}, bf16[128,8,512]{2,1,0:T(8,128)(2,1)S(1)}, u32[]{:S(2)}) copy-start(bf16[128,8,512]{2,1,0:T(8,128)(2,1)S(1)} %all-to-all-done.2.tok_hbm) | copy-start | bytes 3145732
  57.8 26.4 %all-to-all-start = ((bf16[128,8,512]{2,1,0:T(8,128)(2,1)}), bf16[128,8,512]{2,1,0:T(8,128)(2,1)S(1)}, u32[]{:S(2)}, u32[]{:S(2)}) async-start(bf16[128,8,512]{2,1,0:T(8,128)(2,1)} %bitcast.25), calls=%async_computation | async-start | bytes 2097152 | tf_op jit(solution)/shard_map/all_to_all | solution.py:557
  84.3 9.8 %copy-start.6 = (bf16[128,8,512]{2,1,0:T(8,128)(2,1)}, bf16[128,8,512]{2,1,0:T(8,128)(2,1)S(1)}, u32[]{:S(2)}) copy-start(bf16[128,8,512]{2,1,0:T(8,128)(2,1)S(1)} %all-to-all-done.tok_hbm) | copy-start | bytes 3145732
  84.3 30.6 %all-to-all-start.3 = ((bf16[128,8,512]{2,1,0:T(8,128)(2,1)}), bf16[128,8,512]{2,1,0:T(8,128)(2,1)S(1)}, u32[]{:S(2)}, u32[]{:S(2)}) async-start(bf16[128,8,512]{2,1,0:T(8,128)(2,1)} %middle.3), calls=%async_computation.3 | async-start | bytes 2097152 | tf_op jit(solution)/shard_map/all_to_all | solution.py:559
  114.9 10.8 %copy-start = (bf16[128,64,128]{2,1,0:T(8,128)(2,1)S(1)}, bf16[128,64,128]{2,1,0:T(8,128)(2,1)}, u32[]{:S(2)}) copy-start(bf16[128,64,128]{2,1,0:T(8,128)(2,1)} %x_hbm.3) | copy-start | bytes 6291460
  114.9 1.0 copy-start.1
  115.8 28.7 %all-to-all-start.1 = ((bf16[128,8,512]{2,1,0:T(8,128)(2,1)}), bf16[128,8,512]{2,1,0:T(8,128)(2,1)S(1)}, u32[]{:S(2)}, u32[]{:S(2)}) async-start(bf16[128,8,512]{2,1,0:T(8,128)(2,1)} %middle.2), calls=%async_computation.1 | async-start | bytes 2097152 | tf_op jit(solution)/shard_map/all_to_all | solution.py:560
  125.6 1.2 copy-start.2
  126.9 1.0 copy-start.3
  144.5 1.0 copy-start.4

commit v2 on v1

--- a/solution.py
+++ b/solution.py
@@ -31,7 +31,6 @@
 MLP_PART = 256
 GROUP = 4
 CONV_ONE, CONV_TWO, MERGE = 9, 8, 8
-LIMIT = 60 << 20
 
 
 def gelu(v):
@@ -245,10 +244,10 @@
 def front(blocks, place, x, left, right, ends, c1, c2, wm):
     vmem = pl.BlockSpec(memory_space=pltpu.VMEM)
     hbm = pl.BlockSpec(memory_space=pltpu.HBM)
-    args = (x, left, right) + tuple(ends) + (c1, c2, wm)
+    args = (held(x), left, right) + tuple(ends) + (c1, c2, wm)
     out = pl.pallas_call(
         functools.partial(front_kernel, blocks),
-        out_shape=jax.ShapeDtypeStruct((16, 4, 2, 8, LATENT), jnp.bfloat16),
+        out_shape=pltpu.HBM((16, 4, 2, 8, LATENT), jnp.bfloat16),
         in_specs=[pl.BlockSpec(memory_space=pltpu.SMEM), hbm]
         + [vmem] * (2 + len(ends))
         + [hbm] * 3,
@@ -269,7 +268,7 @@
             pltpu.VMEM((LATENT, LATENT), jnp.bfloat16),
             pltpu.SemaphoreType.DMA((9,)),
         ],
-        compiler_params=pltpu.CompilerParams(vmem_limit_bytes=LIMIT),
+        compiler_params=pltpu.CompilerParams(vmem_limit_bytes=36 << 20),
         cost_estimate=pl.CostEstimate(
             flops=8_000_000_000, transcendentals=1_100_000, bytes_accessed=5_000_000
         ),
@@ -284,8 +283,56 @@
     return center * lax.rsqrt(spread + EPSILON) * gain
 
 
+def attend(projected, qgain_ref):
+    def scaled(part):
+        heads = part.reshape(NUM_HEADS, HEAD_WIDTH, 256)
+        square = jnp.mean(heads * heads, axis=1, keepdims=True)
+        return (heads * lax.rsqrt(jnp.maximum(square, FLOOR))).reshape(LATENT, 256)
+
+    qgain = jnp.concatenate([qgain_ref[...], qgain_ref[...]], axis=-1)
+    queries = (scaled(projected[0:LATENT]) * qgain).astype(jnp.bfloat16)
+    keys = scaled(projected[LATENT : 2 * LATENT]).T.astype(jnp.bfloat16)
+    values = projected[2 * LATENT :].astype(jnp.bfloat16)
+    blank = jnp.zeros((HEAD_WIDTH, 256), jnp.bfloat16)
+    row = lax.broadcasted_iota(jnp.int32, (16, 256), 0)
+    marks = [jnp.where(row == i, 1.0, 0.0).astype(jnp.bfloat16) for i in range(GROUP)]
+    attended = []
+    for group in range(NUM_HEADS // GROUP):
+        heads = [
+            slice((GROUP * group + i) * HEAD_WIDTH, (GROUP * group + i + 1) * HEAD_WIDTH)
+            for i in range(GROUP)
+        ]
+        right = jnp.concatenate(
+            [
+                jnp.concatenate([queries[heads[i]] if k == i else blank for k in range(GROUP)], axis=0)
+                for i in range(GROUP)
+            ],
+            axis=1,
+        )
+        scores = jnp.dot(
+            keys[:, group * GROUP * 32 : (group + 1) * GROUP * 32], right, preferred_element_type=jnp.float32
+        )
+        expon = jnp.exp2(scores).astype(jnp.bfloat16)
+        left = jnp.concatenate(
+            [
+                jnp.concatenate(
+                    [values[heads[i]] if k == i else blank for k in range(GROUP)] + [marks[i]],
+                    axis=0,
+                )
+                for i in range(GROUP)
+            ],
+            axis=1,
+        )
+        stacked = jnp.concatenate([expon[:, 256 * i : 256 * (i + 1)] for i in range(GROUP)], axis=0)
+        both = jnp.dot(left, stacked, preferred_element_type=jnp.float32)
+        inverse = 1.0 / both[32 * GROUP : 32 * GROUP + 8]
+        for i in range(GROUP):
+            attended.append(both[32 * i : 32 * (i + 1)] * inverse[i : i + 1])
+    return jnp.concatenate(attended, axis=0).T.astype(jnp.bfloat16)
+
+
 def middle_kernel(
-    tok_hbm,
+    tok_ref,
     gains_ref,
     qgain_ref,
     win_hbm,
@@ -307,30 +354,23 @@
         pltpu.make_async_copy(source, target, sems.at[i])
         for i, (source, target) in enumerate(zip(sources, targets))
     ]
-    fills = [
-        pltpu.make_async_copy(
-            tok_hbm.at[pl.ds(32 * i, 32)], staged.at[pl.ds(32 * i, 32)], sems.at[3 + i]
-        )
-        for i in range(4)
-    ]
     parts = [
         pltpu.make_async_copy(
             win_hbm.at[pl.ds(LATENT * i, LATENT)], win_ref.at[pl.ds(LATENT * i, LATENT)], sems.at[7 + i]
         )
         for i in range(3)
     ]
-    for load in fills + parts + loads:
+    for load in parts + loads:
         load.start()
-    for i, fill in enumerate(fills):
-        fill.wait()
-        held = staged[32 * i : 32 * (i + 1)].reshape(256, LATENT).astype(jnp.float32)
+    for i in range(4):
+        some = tok_ref[32 * i : 32 * (i + 1)].reshape(256, LATENT).astype(jnp.float32)
         for q in range(4):
-            cells[q, 256 * i : 256 * (i + 1)] = held[:, q * 128 : (q + 1) * 128]
+            cells[q, 256 * i : 256 * (i + 1)] = some[:, q * 128 : (q + 1) * 128]
     for part in parts:
         part.wait()
 
-    def window(step, carry):
-        places = [pl.ds(step + WINDOWS * p, 128, stride=8) for p in range(2)]
+    def pair(step, carry):
+        places = [pl.ds(2 * step + w + WINDOWS * p, 128, stride=8) for w in range(2) for p in range(2)]
         tokens = jnp.concatenate(
             [jnp.concatenate([cells[q, place, :] for q in range(4)], axis=-1) for place in places],
             axis=0,
@@ -339,64 +379,21 @@
         projected = lax.dot_general(
             win_ref[...], normed, (((1,), (1,)), ((), ())), preferred_element_type=jnp.float32
         )
-
-        def scaled(part):
-            heads = part.reshape(NUM_HEADS, HEAD_WIDTH, 256)
-            square = jnp.mean(heads * heads, axis=1, keepdims=True)
-            return (heads * lax.rsqrt(jnp.maximum(square, FLOOR))).reshape(LATENT, 256)
-
-        qgain = jnp.concatenate([qgain_ref[...], qgain_ref[...]], axis=-1)
-        queries = (scaled(projected[0:LATENT]) * qgain).astype(jnp.bfloat16)
-        keys = scaled(projected[LATENT : 2 * LATENT]).T.astype(jnp.bfloat16)
-        values = projected[2 * LATENT :].astype(jnp.bfloat16)
-        blank = jnp.zeros((HEAD_WIDTH, 256), jnp.bfloat16)
-        row = lax.broadcasted_iota(jnp.int32, (16, 256), 0)
-        marks = [jnp.where(row == i, 1.0, 0.0).astype(jnp.bfloat16) for i in range(GROUP)]
-        attended = []
-        for group in range(NUM_HEADS // GROUP):
-            heads = [
-                slice((GROUP * group + i) * HEAD_WIDTH, (GROUP * group + i + 1) * HEAD_WIDTH)
-                for i in range(GROUP)
-            ]
-            right = jnp.concatenate(
-                [
-                    jnp.concatenate([queries[heads[i]] if k == i else blank for k in range(GROUP)], axis=0)
-                    for i in range(GROUP)
-                ],
-                axis=1,
-            )
-            scores = jnp.dot(
-                keys[:, group * GROUP * 32 : (group + 1) * GROUP * 32], right, preferred_element_type=jnp.float32
-            )
-            expon = jnp.exp2(scores).astype(jnp.bfloat16)
-            left = jnp.concatenate(
-                [
-                    jnp.concatenate(
-                        [values[heads[i]] if k == i else blank for k in range(GROUP)] + [marks[i]],
-                        axis=0,
-                    )
-                    for i in range(GROUP)
-                ],
-                axis=1,
-            )
-            stacked = jnp.concatenate([expon[:, 256 * i : 256 * (i + 1)] for i in range(GROUP)], axis=0)
-            both = jnp.dot(left, stacked, preferred_element_type=jnp.float32)
-            inverse = 1.0 / both[32 * GROUP : 32 * GROUP + 8]
-            for i in range(GROUP):
-                attended.append(both[32 * i : 32 * (i + 1)] * inverse[i : i + 1])
-        attended = jnp.concatenate(attended, axis=0).T.astype(jnp.bfloat16)
+        attended = jnp.concatenate(
+            [attend(projected[:, 256 * w : 256 * (w + 1)], qgain_ref) for w in range(2)], axis=0
+        )
 
         @pl.when(step == 0)
         def _():
             loads[0].wait()
 
         mixed = tokens + jnp.dot(attended, wout_ref[...], preferred_element_type=jnp.float32)
-        for p in range(2):
+        for at, place in enumerate(places):
             for q in range(4):
-                cells[q, places[p], :] = mixed[128 * p : 128 * (p + 1), 128 * q : 128 * (q + 1)]
+                cells[q, place, :] = mixed[128 * at : 128 * (at + 1), 128 * q : 128 * (q + 1)]
         return carry
 
-    lax.fori_loop(0, WINDOWS, window, 0, unroll=2)
+    lax.fori_loop(0, WINDOWS // 2, pair, 0)
     loads[1].wait()
     loads[2].wait()
     stores = []
@@ -426,8 +423,8 @@
     hbm = pl.BlockSpec(memory_space=pltpu.HBM)
     return pl.pallas_call(
         middle_kernel,
-        out_shape=jax.ShapeDtypeStruct((128, 8, LATENT), jnp.bfloat16),
-        in_specs=[hbm] + [vmem] * 2 + [hbm] * 4,
+        out_shape=pltpu.HBM((128, 8, LATENT), jnp.bfloat16),
+        in_specs=[vmem] * 3 + [hbm] * 4,
         out_specs=hbm,
         scratch_shapes=[
             pltpu.VMEM((4, 1024, 128), jnp.float32),
@@ -438,7 +435,7 @@
             pltpu.VMEM((MLP_WIDTH, LATENT), jnp.bfloat16),
             pltpu.SemaphoreType.DMA((10 + 1024 // MLP_ROWS,)),
         ],
-        compiler_params=pltpu.CompilerParams(vmem_limit_bytes=LIMIT),
+        compiler_params=pltpu.CompilerParams(vmem_limit_bytes=36 << 20),
         cost_estimate=pl.CostEstimate(
             flops=16_000_000_000, transcendentals=6_000_000, bytes_accessed=9_000_000
         ),
@@ -492,6 +489,10 @@
         ),
         name="back_inner" if blocks == INNER else "back_outer",
     )(*args)
+
+
+def held(array):
+    return pltpu.with_memory_space_constraint(array, pltpu.HBM)
 
 
 def from_before(cells, axis):
@@ -550,17 +551,20 @@
     exchange = functools.partial(
         lax.all_to_all, axis_name=("lat", "lon"), split_axis=0, concat_axis=0, tiled=True
     )
-    inner = front(INNER, place, x, left, right, (), conv_one, conv_two, merge_weight)
-    inner, top, bottom, win = lax.optimization_barrier((inner, top, bottom, win))
+    kernels = tuple(held(w) for w in (conv_one, conv_two, merge_weight))
+    inner = front(INNER, place, x, left, right, (), *kernels)
+    inner, top, bottom, win, qgain = lax.optimization_barrier((inner, top, bottom, win, qgain))
     inner = exchange(inner)
-    outer = front(OUTER, place, x, left, right, (top, bottom), conv_one, conv_two, merge_weight)
+    outer = front(OUTER, place, x, left, right, (top, bottom), *kernels)
     outer = exchange(outer)
-    weights = (norm_gains, qgain, win, attention_out, dense_in, dense_out)
+    weights = (norm_gains, qgain) + tuple(
+        held(w) for w in (win, attention_out, dense_in, dense_out)
+    )
     inner = exchange(middle(inner, *weights))
     outer = exchange(middle(outer, *weights))
     field = x.reshape(2, 64, COLS, CHANNELS)
-    result = back(INNER, inner, field, expand_weight, None)
-    result = back(OUTER, outer, field, expand_weight, result)
+    result = back(INNER, held(inner), field, held(expand_weight), None)
+    result = back(OUTER, outer, field, held(expand_weight), result)
     return result.reshape(ROWS, COLS, CHANNELS)
 
 

time: 148 us -> 137 us (0.926)
  Pallas kernels: 63.4 us -> 55.2 us
  waiting for transfers between devices: 25.7 us -> 33.1 us
  starting transfers between devices: 47.7 us -> 41.8 us
  local copies, waits for them, and re-layouts: 9.7 us -> 5.68 us
    pallas_call x4, Pallas kernels: 59.6 us -> 49.2 us  [the longest x2 31.7 us: middle(): pl.pallas_call(middle_kernel, out_shape=pltpu.HBM((128, 8, LATENT), jnp.b...]
    unnamed x27 -> x9, local copies, waits for them, and re-layouts: 6.91 us -> 3.62 us
    all_to_all x1, waiting for transfers between devices: 0.01 us -> 3.07 us  [per_device(): inner = exchange(middle(inner, *weights))]
    all_to_all x1, waiting for transfers between devices: 0.01 us -> 3.07 us  [per_device(): outer = exchange(outer)]
    all_to_all x1, starting transfers between devices: 9.78 us -> 6.73 us  [per_device(): inner = exchange(middle(inner, *weights))]
    all_to_all x1, starting transfers between devices: 9.76 us -> 6.71 us  [per_device(): outer = exchange(middle(outer, *weights))]
    pallas_call x2, Pallas kernels: 3.79 us -> 5.97 us  [back(): pl.pallas_call(back_kernel, out_shape=jax.ShapeDtypeStruct((2, 64, COLS,...]
  transfers between devices with their start and end apart: 8 -> 8, of which waited for: 3 -> 5; matrix products, arithmetic and copies ran while one was open for 3% -> 3% of each run, Pallas kernels for 42% -> 38%
where the time goes in v2:
time: 137 us
  Pallas kernels  55.2 us (40%)
  starting transfers between devices  41.8 us (31%)
  waiting for transfers between devices  33.1 us (24%)
  local copies, waits for them, and re-layouts  5.68 us (4%)
    pallas_call x2, Pallas kernels, middle(): pl.pallas_call(middle_kernel, out_shape=pltpu.HBM((128, 8, LATENT), jnp.b...  31.7 us
    pallas_call x2, Pallas kernels, front(): pl.pallas_call(functools.partial(front_kernel, blocks), out_shape=pltpu.H...  17.5 us
    all_to_all x1, waiting for transfers between devices, per_device(): outer = exchange(middle(outer, *weights))  15.9 us
    all_to_all x1, starting transfers between devices, per_device(): inner = exchange(inner)  10.3 us
    all_to_all x1, waiting for transfers between devices, per_device(): inner = exchange(inner)  10.2 us
    ppermute x2, starting transfers between devices, from_before(): return lax.ppermute(cells, axis, [(i, i + 1) for i in range(ends)])  10 us
    all_to_all x1, starting transfers between devices, per_device(): inner = exchange(middle(inner, *weights))  6.73 us
    all_to_all x1, starting transfers between devices, per_device(): outer = exchange(middle(outer, *weights))  6.71 us
  transfers between devices with their start and end apart: 8, of which 5 were waited for; matrix products, arithmetic and copies ran while one was open for 3% of the time, Pallas kernels for 38%

profile of v2, /device:TPU:1, one launch (start us, length us, event | category | flops | bytes accessed | tf_op | source)
XLA Modules:
  0.0 136.8 jit_solution(5032535760467046920)
XLA Ops:
  0.0 1.1 fusion.1
  1.2 6.9 %collective-permute-start = (bf16[2,128,128]{2,1,0:T(8,128)(2,1)S(1)}, bf16[2,128,128]{2,1,0:T(8,128)(2,1)S(1)}, u32[]{:S(2)}, u32[]{:S(2)}) collective-permute-start(bf16[2,128,128]{2,1,0:T(8,128)(2,1)S(1)} %bitcast.28), channel_id=1, source_target_pairs={{0,1},{1,2},{2,3},{3,4},{4,5},{5,6},{6,7},{7,8},{8,9},{9,10},{10,1... | collective-permute-start | bytes 196616 | tf_op jit(solution)/shard_map/ppermute | solution.py:500
  8.1 1.9 %collective-permute-start.1 = (bf16[2,128,128]{2,1,0:T(8,128)(2,1)S(1)}, bf16[2,128,128]{2,1,0:T(8,128)(2,1)S(1)}, u32[]{:S(2)}, u32[]{:S(2)}) collective-permute-start(bf16[2,128,128]{2,1,0:T(8,128)(2,1)S(1)} %bitcast.29), channel_id=1, source_target_pairs={{1,0},{2,1},{3,2},{4,3},{5,4},{6,5},{7,6},{8,7},{9,8},{10,9},{11,1... | collective-permute-start | bytes 196616 | tf_op jit(solution)/shard_map/ppermute | solution.py:505
  10.0 0.8 fusion
  10.8 0.8 multiply_multiply_fusion
  11.6 2.6 %copy.14 = bf16[512,1536]{0,1:T(8,128)(2,1)} copy(bf16[512,1536]{1,0:T(8,128)(2,1)} %param.15) | data formatting | bytes 3145728 | tf_op args[5]
  14.2 0.1 pad_add_fusion.edge_ref
  14.2 0.0 collective-permute-done.left_ref
  14.3 0.9 collective-permute-done.1.right_ref
  15.2 3.1 %collective-permute-start.2 = (bf16[136,128]{1,0:T(8,128)(2,1)S(1)}, bf16[136,128]{1,0:T(8,128)(2,1)S(1)}, u32[]{:S(2)}, u32[]{:S(2)}) collective-permute-start(bf16[136,128]{1,0:T(8,128)(2,1)S(1)} %pad_maximum_fusion), channel_id=1, source_target_pairs={{0,16},{16,32},{32,48},{48,64},{64,80},{80,96},{96,112},{1,17},{17... | collective-permute-start | bytes 104456 | tf_op jit(solution)/shard_map/ppermute | solution.py:500
  18.3 1.3 collective-permute-start.3
  19.6 8.8 %front_inner.1 = bf16[16,4,2,8,512]{4,3,2,1,0:T(8,128)(2,1)} custom-call(s32[4]{0:T(128)S(1)} %pad_add_fusion.edge_ref, bf16[128,64,128]{2,1,0:T(8,128)(2,1)} %x_hbm.3, bf16[2,128,128]{2,1,0:T(8,128)(2,1)S(1)} %collective-permute-done.left_ref, bf16[2,128,128]{2,1,0:T(8,128)(2,1)S(1)} %collective-permute-done.1.right_ref, bf16[3,3,128,128]{3,2,1,0:T(8,128)(2,1)} %rest_2_.3, ...), custom_call_target="tpu_custom_call" | custom-call | flops 8000000000 | bytes 5000000 | tf_op jit(solution)/shard_map/front_inner/pallas_call | solution.py:248
  28.4 0.0 collective-permute-done.2.rest_0_
  28.4 0.0 collective-permute-done.3.rest_1_
  28.4 0.1 broadcast_in_dim.2.qgain_ref
  28.6 10.3 %all-to-all-start.2 = ((bf16[128,8,512]{2,1,0:T(8,128)(2,1)}), bf16[128,8,512]{2,1,0:T(8,128)(2,1)S(1)}, u32[]{:S(2)}, u32[]{:S(2)}) async-start(bf16[128,8,512]{2,1,0:T(8,128)(2,1)} %bitcast.24), calls=%async_computation.2 | async-start | bytes 2097152 | tf_op jit(solution)/shard_map/all_to_all | solution.py:557
  38.9 8.7 %front_outer.1 = bf16[16,4,2,8,512]{4,3,2,1,0:T(8,128)(2,1)} custom-call(s32[4]{0:T(128)S(1)} %pad_add_fusion.edge_ref, bf16[128,64,128]{2,1,0:T(8,128)(2,1)} %x_hbm.3, bf16[2,128,128]{2,1,0:T(8,128)(2,1)S(1)} %collective-permute-done.left_ref, bf16[2,128,128]{2,1,0:T(8,128)(2,1)S(1)} %collective-permute-done.1.right_ref, ...), custom_call_target="tpu_custom_call" | custom-call | flops 8000000000 | bytes 5000000 | tf_op jit(solution)/shard_map/front_outer/pallas_call | solution.py:248
  47.6 0.0 copy-start.1
  47.6 10.2 %all-to-all-done.2.tok_ref = bf16[128,8,512]{2,1,0:T(8,128)(2,1)S(1)} async-done(((bf16[128,8,512]{2,1,0:T(8,128)(2,1)}), bf16[128,8,512]{2,1,0:T(8,128)(2,1)S(1)}, u32[]{:S(2)}, u32[]{:S(2)}) %all-to-all-start.2) | async-done | bytes 1048608 | tf_op jit(solution)/shard_map/all_to_all | solution.py:557
  57.8 4.8 %all-to-all-start = ((bf16[128,8,512]{2,1,0:T(8,128)(2,1)}), bf16[128,8,512]{2,1,0:T(8,128)(2,1)S(1)}, u32[]{:S(2)}, u32[]{:S(2)}) async-start(bf16[128,8,512]{2,1,0:T(8,128)(2,1)} %bitcast.25), calls=%async_computation | async-start | bytes 2097152 | tf_op jit(solution)/shard_map/all_to_all | solution.py:559
  62.6 0.0 copy-done.1
  62.7 15.8 %middle.3 = bf16[128,8,512]{2,1,0:T(8,128)(2,1)} custom-call(bf16[128,8,512]{2,1,0:T(8,128)(2,1)S(1)} %all-to-all-done.2.tok_ref, f32[4,512]{1,0:T(4,128)S(1)} %copy-done.1, f32[512,128]{1,0:T(8,128)S(1)} %broadcast_in_dim.2.qgain_ref, bf16[1536,512]{1,0:T(8,128)(2,1)} %bitcast.22, bf16[512,512]{1,0:T(8,128)(2,1)} %wout_hbm.3, bf16[512,2048]{1,0:T(8,128)(2,1)} %wi_hbm.3, ...), custom_call_target="tpu_custom_call" | custom-call | flops 16000000000 | bytes 9000000 | tf_op jit(solution)/shard_map/middle/pallas_call | solution.py:424
  78.5 3.1 %all-to-all-done.tok_ref = bf16[128,8,512]{2,1,0:T(8,128)(2,1)S(1)} async-done(((bf16[128,8,512]{2,1,0:T(8,128)(2,1)}), bf16[128,8,512]{2,1,0:T(8,128)(2,1)S(1)}, u32[]{:S(2)}, u32[]{:S(2)}) %all-to-all-start) | async-done | bytes 1048608 | tf_op jit(solution)/shard_map/all_to_all | solution.py:559
  81.6 6.7 %all-to-all-start.3 = ((bf16[128,8,512]{2,1,0:T(8,128)(2,1)}), bf16[128,8,512]{2,1,0:T(8,128)(2,1)S(1)}, u32[]{:S(2)}, u32[]{:S(2)}) async-start(bf16[128,8,512]{2,1,0:T(8,128)(2,1)} %middle.3), calls=%async_computation.3 | async-start | bytes 2097152 | tf_op jit(solution)/shard_map/all_to_all | solution.py:563
  88.3 15.8 %middle.2 = bf16[128,8,512]{2,1,0:T(8,128)(2,1)} custom-call(bf16[128,8,512]{2,1,0:T(8,128)(2,1)S(1)} %all-to-all-done.tok_ref, f32[4,512]{1,0:T(4,128)S(1)} %copy-done.1, f32[512,128]{1,0:T(8,128)S(1)} %broadcast_in_dim.2.qgain_ref, bf16[1536,512]{1,0:T(8,128)(2,1)} %bitcast.23, bf16[512,512]{1,0:T(8,128)(2,1)} %wout_hbm.3, bf16[512,2048]{1,0:T(8,128)(2,1)} %wi_hbm.3, ...), custom_call_target="tpu_custom_call" | custom-call | flops 16000000000 | bytes 9000000 | tf_op jit(solution)/shard_map/middle/pallas_call | solution.py:424
  104.1 0.0 copy-start
  104.1 3.1 %all-to-all-done.3.cells_ref = bf16[128,8,512]{2,1,0:T(8,128)(2,1)S(1)} async-done(((bf16[128,8,512]{2,1,0:T(8,128)(2,1)}), bf16[128,8,512]{2,1,0:T(8,128)(2,1)S(1)}, u32[]{:S(2)}, u32[]{:S(2)}) %all-to-all-start.3) | async-done | bytes 1048608 | tf_op jit(solution)/shard_map/all_to_all | solution.py:563
  107.2 0.0 copy-start.2
  107.2 1.0 copy-done.2
  108.2 6.7 %all-to-all-start.1 = ((bf16[128,8,512]{2,1,0:T(8,128)(2,1)}), bf16[128,8,512]{2,1,0:T(8,128)(2,1)S(1)}, u32[]{:S(2)}, u32[]{:S(2)}) async-start(bf16[128,8,512]{2,1,0:T(8,128)(2,1)} %middle.2), calls=%async_computation.1 | async-start | bytes 2097152 | tf_op jit(solution)/shard_map/all_to_all | solution.py:564
  114.9 0.0 copy-done
  114.9 3.1 %back_inner.1.rest_0_ = bf16[2,64,64,128]{3,2,1,0:T(8,128)(2,1)} custom-call(bf16[128,8,512]{2,1,0:T(8,128)(2,1)} %copy-done.2, bf16[2,64,64,128]{3,2,1,0:T(8,128)(2,1)S(1)} %bitcast.20, bf16[512,512]{1,0:T(8,128)(2,1)} %we_ref.3), custom_call_target="tpu_custom_call" | custom-call | flops 540000000 | bytes 4000000 | tf_op jit(solution)/shard_map/back_inner/pallas_call | solution.py:478
  118.0 15.9 %all-to-all-done.1.cells_ref = bf16[128,8,512]{2,1,0:T(8,128)(2,1)S(1)} async-done(((bf16[128,8,512]{2,1,0:T(8,128)(2,1)}), bf16[128,8,512]{2,1,0:T(8,128)(2,1)S(1)}, u32[]{:S(2)}, u32[]{:S(2)}) %all-to-all-start.1) | async-done | bytes 1048608 | tf_op jit(solution)/shard_map/all_to_all | solution.py:564
  133.9 2.9 %back_outer.1 = bf16[2,64,64,128]{3,2,1,0:T(8,128)(2,1)} custom-call(bf16[128,8,512]{2,1,0:T(8,128)(2,1)S(1)} %all-to-all-done.1.cells_ref, bf16[2,64,64,128]{3,2,1,0:T(8,128)(2,1)S(1)} %bitcast.21, bf16[512,512]{1,0:T(8,128)(2,1)} %we_ref.3, bf16[2,64,64,128]{3,2,1,0:T(8,128)(2,1)} %back_inner.1.rest_0_), custom_call_target="tpu_custom_call", output_to_operand_aliasing={{}: (3, {})} | custom-call | flops 540000000 | bytes 4000000 | tf_op jit(solution)/shard_map/back_outer/pallas_call | solution.py:478
  (6 shorter events, 0.1 us)
Async XLA Ops:
  1.2 13.1 %collective-permute-start = (bf16[2,128,128]{2,1,0:T(8,128)(2,1)S(1)}, bf16[2,128,128]{2,1,0:T(8,128)(2,1)S(1)}, u32[]{:S(2)}, u32[]{:S(2)}) collective-permute-start(bf16[2,128,128]{2,1,0:T(8,128)(2,1)S(1)} %bitcast.28), channel_id=1, source_target_pairs={{0,1},{1,2},{2,3},{3,4},{4,5},{5,6},{6,7},{7,8},{8,9},{9,10},{10,1... | collective-permute-start | bytes 196616 | tf_op jit(solution)/shard_map/ppermute | solution.py:500
  8.1 7.1 %collective-permute-start.1 = (bf16[2,128,128]{2,1,0:T(8,128)(2,1)S(1)}, bf16[2,128,128]{2,1,0:T(8,128)(2,1)S(1)}, u32[]{:S(2)}, u32[]{:S(2)}) collective-permute-start(bf16[2,128,128]{2,1,0:T(8,128)(2,1)S(1)} %bitcast.29), channel_id=1, source_target_pairs={{1,0},{2,1},{3,2},{4,3},{5,4},{6,5},{7,6},{8,7},{9,8},{10,9},{11,1... | collective-permute-start | bytes 196616 | tf_op jit(solution)/shard_map/ppermute | solution.py:505
  15.2 13.2 %collective-permute-start.2 = (bf16[136,128]{1,0:T(8,128)(2,1)S(1)}, bf16[136,128]{1,0:T(8,128)(2,1)S(1)}, u32[]{:S(2)}, u32[]{:S(2)}) collective-permute-start(bf16[136,128]{1,0:T(8,128)(2,1)S(1)} %pad_maximum_fusion), channel_id=1, source_target_pairs={{0,16},{16,32},{32,48},{48,64},{64,80},{80,96},{96,112},{1,17},{17... | collective-permute-start | bytes 104456 | tf_op jit(solution)/shard_map/ppermute | solution.py:500
  18.3 10.1 %collective-permute-start.3 = (bf16[136,128]{1,0:T(8,128)(2,1)S(1)}, bf16[136,128]{1,0:T(8,128)(2,1)S(1)}, u32[]{:S(2)}, u32[]{:S(2)}) collective-permute-start(bf16[136,128]{1,0:T(8,128)(2,1)S(1)} %pad_maximum_fusion.1), channel_id=1, source_target_pairs={{16,0},{32,16},{48,32},{64,48},{80,64},{96,80},{112,96},{17,1},{33... | collective-permute-start | bytes 104456 | tf_op jit(solution)/shard_map/ppermute | solution.py:505
  28.6 29.2 %all-to-all-start.2 = ((bf16[128,8,512]{2,1,0:T(8,128)(2,1)}), bf16[128,8,512]{2,1,0:T(8,128)(2,1)S(1)}, u32[]{:S(2)}, u32[]{:S(2)}) async-start(bf16[128,8,512]{2,1,0:T(8,128)(2,1)} %bitcast.24), calls=%async_computation.2 | async-start | bytes 2097152 | tf_op jit(solution)/shard_map/all_to_all | solution.py:557
  47.6 15.0 %copy-start.1 = (f32[4,512]{1,0:T(4,128)S(1)}, f32[4,512]{1,0:T(4,128)}, u32[]{:S(2)}) copy-start(f32[4,512]{1,0:T(4,128)} %gains_ref.3) | copy-start | bytes 24580
  57.8 23.8 %all-to-all-start = ((bf16[128,8,512]{2,1,0:T(8,128)(2,1)}), bf16[128,8,512]{2,1,0:T(8,128)(2,1)S(1)}, u32[]{:S(2)}, u32[]{:S(2)}) async-start(bf16[128,8,512]{2,1,0:T(8,128)(2,1)} %bitcast.25), calls=%async_computation | async-start | bytes 2097152 | tf_op jit(solution)/shard_map/all_to_all | solution.py:559
  81.6 25.7 %all-to-all-start.3 = ((bf16[128,8,512]{2,1,0:T(8,128)(2,1)}), bf16[128,8,512]{2,1,0:T(8,128)(2,1)S(1)}, u32[]{:S(2)}, u32[]{:S(2)}) async-start(bf16[128,8,512]{2,1,0:T(8,128)(2,1)} %middle.3), calls=%async_computation.3 | async-start | bytes 2097152 | tf_op jit(solution)/shard_map/all_to_all | solution.py:563
  104.1 10.8 %copy-start = (bf16[128,64,128]{2,1,0:T(8,128)(2,1)S(1)}, bf16[128,64,128]{2,1,0:T(8,128)(2,1)}, u32[]{:S(2)}) copy-start(bf16[128,64,128]{2,1,0:T(8,128)(2,1)} %x_hbm.3) | copy-start | bytes 6291460
  107.2 1.0 copy-start.2
  108.2 25.6 %all-to-all-start.1 = ((bf16[128,8,512]{2,1,0:T(8,128)(2,1)}), bf16[128,8,512]{2,1,0:T(8,128)(2,1)S(1)}, u32[]{:S(2)}, u32[]{:S(2)}) async-start(bf16[128,8,512]{2,1,0:T(8,128)(2,1)} %middle.2), calls=%async_computation.1 | async-start | bytes 2097152 | tf_op jit(solution)/shard_map/all_to_all | solution.py:564

commit v3 on v2

--- a/solution.py
+++ b/solution.py
@@ -59,8 +59,10 @@
         top_ref, bottom_ref = rest[:2]
         rest = rest[2:]
     weights_hbm, out_hbm = rest[:3], rest[3]
-    stage, sides, xab, firsts, fab, seconds, out_ref, x_ref = rest[4:12]
-    c1_ref, c2_ref, w1_ref, w2_ref, wm_ref, sems = rest[12:]
+    stage, sides, xab, firsts, fab, seconds, out_ref = rest[4:11]
+    x_ref, c1_ref, c2_ref, wm_ref, w1_ref, w2_ref, sems = rest[11:]
+    if blocks == INNER:
+        c1_ref, c2_ref = weights_hbm[:2]
     lat, lon = edge_ref[0], edge_ref[1]
     keep = [
         jnp.where(inside, 1.0, 0.0)
@@ -73,22 +75,25 @@
         ]
         for block in blocks
     ]
-    fills = [
-        [
-            pltpu.make_async_copy(
-                x_hbm.at[pl.ds(low, high - low)],
-                x_ref.at[2 * at + p, pl.ds(0, high - low)],
-                sems.at[2 + 2 * at + p],
-            )
-            for p, (low, high, _) in enumerate(pair)
-        ]
-        for at, pair in enumerate(spans)
-    ]
     loads = [
         pltpu.make_async_copy(source, target, sems.at[6 + i])
         for i, (source, target) in enumerate(zip(weights_hbm, (c1_ref, c2_ref, wm_ref)))
-    ]
-    for copy in fills[0] + loads[:1] + fills[1] + loads[1:]:
+        if source is not target
+    ]
+    fills = []
+    if blocks == OUTER:
+        fills = [
+            [
+                pltpu.make_async_copy(
+                    x_hbm.at[pl.ds(low, high - low)],
+                    x_ref.at[2 * at + p, pl.ds(0, high - low)],
+                    sems.at[2 + 2 * at + p],
+                )
+                for p, (low, high, _) in enumerate(pair)
+            ]
+            for at, pair in enumerate(spans)
+        ]
+    for copy in sum(fills[:1], []) + loads[:1] + sum(fills[1:], []) + loads[1:]:
         copy.start()
     stores = [
         pltpu.make_async_copy(
@@ -105,11 +110,14 @@
         for p in range(2):
             low, high, skip = spans[at][p]
             count = high - low
-            fills[at][p].wait()
-
-            def place(r, carry, at=at, p=p, skip=skip):
+            if blocks == OUTER:
+                fills[at][p].wait()
+
+            source = x_ref.at[2 * at + p] if blocks == OUTER else x_hbm.at[pl.ds(low, count)]
+
+            def place(r, carry, p=p, skip=skip, source=source):
                 to = pl.multiple_of((p * STAGE_ROWS + skip + r) * STRIDE + LEAD, 8)
-                stage[pl.ds(to, COLS), :] = x_ref[2 * at + p, r].astype(jnp.float32)
+                stage[pl.ds(to, COLS), :] = source[r].astype(jnp.float32)
                 return carry
 
             lax.fori_loop(0, count, place, 0, unroll=2)
@@ -142,7 +150,8 @@
                     [stage[pl.ds(base + k, PAIRS, stride=2), :] for k in (-2, -1, 0, 1)], axis=-1
                 ).astype(jnp.bfloat16)
         if at == 0:
-            loads[0].wait()
+            if blocks == OUTER:
+                loads[0].wait()
             pair_columns(c1_ref, w1_ref)
         for p in range(2):
             for r0 in range(0, 18, CONV_ONE):
@@ -203,8 +212,8 @@
                     axis=-1,
                 ).astype(jnp.bfloat16)
         if at == 0:
-            loads[1].wait()
-            loads[2].wait()
+            for load in loads[1:] if blocks == OUTER else loads:
+                load.wait()
             pair_columns(c2_ref, w2_ref)
         for p in range(2):
             for r0 in range(0, 16, CONV_TWO):
@@ -244,13 +253,20 @@
 def front(blocks, place, x, left, right, ends, c1, c2, wm):
     vmem = pl.BlockSpec(memory_space=pltpu.VMEM)
     hbm = pl.BlockSpec(memory_space=pltpu.HBM)
-    args = (held(x), left, right) + tuple(ends) + (c1, c2, wm)
+    args = (x, left, right) + tuple(ends) + (c1, c2, wm)
+    far = vmem if blocks == INNER else hbm
+    copies = [
+        pltpu.VMEM((4 if blocks == OUTER else 1, 20, COLS, CHANNELS), jnp.bfloat16),
+        pltpu.VMEM((3, 3, CHANNELS, CHANNELS), jnp.bfloat16),
+        pltpu.VMEM((3, 3, CHANNELS, CHANNELS), jnp.bfloat16),
+        pltpu.VMEM((LATENT, LATENT), jnp.bfloat16),
+    ]
     out = pl.pallas_call(
         functools.partial(front_kernel, blocks),
         out_shape=pltpu.HBM((16, 4, 2, 8, LATENT), jnp.bfloat16),
-        in_specs=[pl.BlockSpec(memory_space=pltpu.SMEM), hbm]
+        in_specs=[pl.BlockSpec(memory_space=pltpu.SMEM), far]
         + [vmem] * (2 + len(ends))
-        + [hbm] * 3,
+        + [far, far, hbm],
         out_specs=hbm,
         scratch_shapes=[
             pltpu.VMEM((2 * STAGE_ROWS * STRIDE, CHANNELS), jnp.float32),
@@ -260,12 +276,11 @@
             pltpu.VMEM((2, 18, PAIRS, 512), jnp.bfloat16),
             pltpu.VMEM((2, 8, PAIRS, LATENT), jnp.bfloat16),
             pltpu.VMEM((16, 4, 2, 8, LATENT), jnp.bfloat16),
-            pltpu.VMEM((4, 20, COLS, CHANNELS), jnp.bfloat16),
-            pltpu.VMEM((3, 3, CHANNELS, CHANNELS), jnp.bfloat16),
-            pltpu.VMEM((3, 3, CHANNELS, CHANNELS), jnp.bfloat16),
+        ]
+        + copies
+        + [
             pltpu.VMEM((1536, 256), jnp.bfloat16),
             pltpu.VMEM((1536, 256), jnp.bfloat16),
-            pltpu.VMEM((LATENT, LATENT), jnp.bfloat16),
             pltpu.SemaphoreType.DMA((9,)),
         ],
         compiler_params=pltpu.CompilerParams(vmem_limit_bytes=36 << 20),
@@ -443,52 +458,96 @@
     )(tokens, gains, qgain, win, wout, wi, wd)
 
 
-def back_kernel(cells_ref, x_ref, we_ref, *rest):
-    out_ref, even, odd = rest[-3:]
-    expanded = jnp.dot(
-        cells_ref[...].reshape(512, LATENT), we_ref[...], preferred_element_type=jnp.float32
-    )
-    for di, held in enumerate((even, odd)):
+def back_cells(cells_ref, x_ref, we_ref, loads, out_ref, even, odd):
+    cells = cells_ref[...].reshape(512, LATENT)
+    for di, side in enumerate((even, odd)):
+        if loads:
+            loads[di].wait()
+        expanded = jnp.dot(
+            cells, we_ref[:, 256 * di : 256 * (di + 1)], preferred_element_type=jnp.float32
+        )
         for dj in range(2):
-            lanes = (2 * di + dj) * CHANNELS
-            held[pl.ds(dj, 512, stride=2), :] = expanded[:, lanes : lanes + CHANNELS]
-    for di, held in enumerate((even, odd)):
+            side[pl.ds(dj, 512, stride=2), :] = expanded[:, dj * CHANNELS : (dj + 1) * CHANNELS]
+    for di, side in enumerate((even, odd)):
         for u in range(8):
-            rows = held[u * 128 : (u + 1) * 128, :].reshape(8, 2, 8, CHANNELS)
+            rows = side[u * 128 : (u + 1) * 128, :].reshape(8, 2, 8, CHANNELS)
             for p in range(2):
                 fine = rows[:, p].reshape(COLS, CHANNELS)
                 old = x_ref[p, 2 * u + di].astype(jnp.float32)
                 out_ref[p, 2 * u + di] = (fine + old).astype(jnp.bfloat16)
 
 
-def back(blocks, cells, x, we, before):
-    step = blocks[1] - blocks[0]
-    fine = pl.BlockSpec((2, 16, COLS, CHANNELS), lambda i: (0, blocks[0] + step * i, 0, 0))
-    specs = [
-        pl.BlockSpec((64, 8, LATENT), lambda i: (i, 0, 0)),
-        fine,
-        pl.BlockSpec((LATENT, LATENT), lambda i: (0, 0), pipeline_mode=pl.Buffered(1)),
-    ]
-    args = (cells, x, we)
-    aliases = {}
-    if before is not None:
-        specs.append(pl.BlockSpec(memory_space=pl.ANY))
-        args += (before,)
-        aliases = {3: 0}
+def back_kernel(blocks, *refs):
+    we_ref, out_ref, even, odd, sems = refs[-5:]
+    expand = [
+        pltpu.make_async_copy(refs[2].at[:, lanes], we_ref.at[:, lanes], sems.at[q])
+        for q, lanes in enumerate((pl.ds(0, 256), pl.ds(256, 256)))
+    ]
+    for load in expand:
+        load.start()
+    if blocks == INNER:
+        cells_ref, x_hbm, we_hbm, out_hbm, kept, x_ref = refs[:6]
+        spans = [(x_hbm, INNER[0], x_ref.at[0]), (x_hbm, INNER[1], x_ref.at[1])]
+        spans += [(x_hbm, OUTER[0], kept.at[0]), (x_hbm, OUTER[1], kept.at[1])]
+        loads = [
+            pltpu.make_async_copy(x.at[:, pl.ds(16 * block, 16)], to, sems.at[4 + i])
+            for i, (x, block, to) in enumerate(spans)
+        ]
+        for load in loads:
+            load.start()
+    else:
+        cells_ref, x_ref, we_hbm, _, out_hbm = refs[:5]
+    stores = []
+    for at, block in enumerate(blocks):
+        if blocks == INNER:
+            loads[at].wait()
+        back_cells(
+            cells_ref.at[pl.ds(64 * at, 64)],
+            x_ref.at[at],
+            we_ref,
+            expand if at == 0 else (),
+            out_ref.at[at],
+            even,
+            odd,
+        )
+        store = pltpu.make_async_copy(
+            out_ref.at[at], out_hbm.at[:, pl.ds(16 * block, 16)], sems.at[2 + at]
+        )
+        store.start()
+        stores.append(store)
+    for store in stores:
+        store.wait()
+    if blocks == INNER:
+        loads[2].wait()
+        loads[3].wait()
+
+
+def back(blocks, cells, *others):
+    vmem = pl.BlockSpec(memory_space=pltpu.VMEM)
+    hbm = pl.BlockSpec(memory_space=pltpu.HBM)
+    field = pltpu.HBM((2, 64, COLS, CHANNELS), jnp.bfloat16)
+    part = pltpu.VMEM((2, 2, 16, COLS, CHANNELS), jnp.bfloat16)
+    first = blocks == INNER
     return pl.pallas_call(
-        back_kernel,
-        out_shape=jax.ShapeDtypeStruct((2, 64, COLS, CHANNELS), jnp.bfloat16),
-        grid=(2,),
-        in_specs=specs,
-        out_specs=fine,
-        scratch_shapes=[pltpu.VMEM((1024, CHANNELS), jnp.float32)] * 2,
-        input_output_aliases=aliases,
+        functools.partial(back_kernel, blocks),
+        out_shape=(field, part) if first else field,
+        in_specs=[vmem, hbm, hbm] if first else [vmem, vmem, hbm, hbm],
+        out_specs=(hbm, vmem) if first else hbm,
+        scratch_shapes=([part] if first else [])
+        + [
+            pltpu.VMEM((LATENT, LATENT), jnp.bfloat16),
+            part,
+            pltpu.VMEM((1024, CHANNELS), jnp.float32),
+            pltpu.VMEM((1024, CHANNELS), jnp.float32),
+            pltpu.SemaphoreType.DMA((8 if first else 4,)),
+        ],
+        input_output_aliases={} if first else {3: 0},
         compiler_params=pltpu.CompilerParams(vmem_limit_bytes=16 << 20),
         cost_estimate=pl.CostEstimate(
             flops=540_000_000, transcendentals=0, bytes_accessed=4_000_000
         ),
-        name="back_inner" if blocks == INNER else "back_outer",
-    )(*args)
+        name="back_inner" if first else "back_outer",
+    )(cells, *others)
 
 
 def held(array):
@@ -551,20 +610,23 @@
     exchange = functools.partial(
         lax.all_to_all, axis_name=("lat", "lon"), split_axis=0, concat_axis=0, tiled=True
     )
-    kernels = tuple(held(w) for w in (conv_one, conv_two, merge_weight))
-    inner = front(INNER, place, x, left, right, (), *kernels)
+    merge = held(merge_weight)
+    inner = front(INNER, place, x, left, right, (), conv_one, conv_two, merge)
     inner, top, bottom, win, qgain = lax.optimization_barrier((inner, top, bottom, win, qgain))
     inner = exchange(inner)
-    outer = front(OUTER, place, x, left, right, (top, bottom), *kernels)
+    outer = front(
+        OUTER, place, held(x), left, right, (top, bottom), held(conv_one), held(conv_two), merge
+    )
     outer = exchange(outer)
     weights = (norm_gains, qgain) + tuple(
         held(w) for w in (win, attention_out, dense_in, dense_out)
     )
     inner = exchange(middle(inner, *weights))
     outer = exchange(middle(outer, *weights))
-    field = x.reshape(2, 64, COLS, CHANNELS)
-    result = back(INNER, held(inner), field, held(expand_weight), None)
-    result = back(OUTER, outer, field, held(expand_weight), result)
+    field = held(x.reshape(2, 64, COLS, CHANNELS))
+    expand = held(expand_weight)
+    result, rest = back(INNER, inner, field, expand)
+    result = back(OUTER, outer, rest, expand, result)
     return result.reshape(ROWS, COLS, CHANNELS)
 
 

time: 137 us -> 136 us (level)
    unnamed x9 -> x11, local copies, waits for them, and re-layouts: 3.62 us -> 2.62 us
where the time goes in v3:
time: 136 us; the launch traced here: 135 us
  Pallas kernels  54.7 us (40%)
  starting transfers between devices  41.8 us (31%)
  waiting for transfers between devices  32.7 us (24%)
  local copies, waits for them, and re-layouts  4.84 us (4%)
    pallas_call x2, Pallas kernels, middle(): pl.pallas_call(middle_kernel, out_shape=pltpu.HBM((128, 8, LATENT), jnp.b...  31.7 us
    pallas_call x2, Pallas kernels, front(): pl.pallas_call(functools.partial(front_kernel, blocks), out_shape=pltpu.H...  16.5 us
    all_to_all x1, waiting for transfers between devices, per_device(): outer = exchange(middle(outer, *weights))  15.4 us
    all_to_all x1, starting transfers between devices, per_device(): inner = exchange(inner)  10.3 us
    all_to_all x1, waiting for transfers between devices, per_device(): inner = exchange(inner)  10.2 us
    ppermute x2, starting transfers between devices, from_before(): return lax.ppermute(cells, axis, [(i, i + 1) for i in range(ends)])  10 us
    all_to_all x1, starting transfers between devices, per_device(): inner = exchange(middle(inner, *weights))  6.74 us
    all_to_all x1, starting transfers between devices, per_device(): outer = exchange(middle(outer, *weights))  6.69 us
  transfers between devices with their start and end apart: 8, of which 5 were waited for; matrix products, arithmetic and copies ran while one was open for 3% of the time, Pallas kernels for 38%

profile of v3, /device:TPU:1, one launch (start us, length us, event | category | flops | bytes accessed | tf_op | source)
XLA Modules:
  0.0 135.3 jit_solution(17223922610915353309)
XLA Ops:
  0.0 0.0 copy-start
  0.0 0.0 copy-start.3
  0.0 0.0 copy-start.2
  0.0 1.3 fusion.1
  1.3 6.9 %collective-permute-start = (bf16[2,128,128]{2,1,0:T(8,128)(2,1)S(1)}, bf16[2,128,128]{2,1,0:T(8,128)(2,1)S(1)}, u32[]{:S(2)}, u32[]{:S(2)}) collective-permute-start(bf16[2,128,128]{2,1,0:T(8,128)(2,1)S(1)} %bitcast.27), channel_id=1, source_target_pairs={{0,1},{1,2},{2,3},{3,4},{4,5},{5,6},{6,7},{7,8},{8,9},{9,10},{10,1... | collective-permute-start | bytes 196616 | tf_op jit(solution)/shard_map/ppermute | solution.py:559
  8.2 1.9 %collective-permute-start.1 = (bf16[2,128,128]{2,1,0:T(8,128)(2,1)S(1)}, bf16[2,128,128]{2,1,0:T(8,128)(2,1)S(1)}, u32[]{:S(2)}, u32[]{:S(2)}) collective-permute-start(bf16[2,128,128]{2,1,0:T(8,128)(2,1)S(1)} %bitcast.28), channel_id=1, source_target_pairs={{1,0},{2,1},{3,2},{4,3},{5,4},{6,5},{7,6},{8,7},{9,8},{10,9},{11,1... | collective-permute-start | bytes 196616 | tf_op jit(solution)/shard_map/ppermute | solution.py:564
  10.2 0.8 fusion
  11.0 0.8 multiply_multiply_fusion
  11.7 2.6 %copy.14 = bf16[512,1536]{0,1:T(8,128)(2,1)} copy(bf16[512,1536]{1,0:T(8,128)(2,1)} %param.15) | data formatting | bytes 3145728 | tf_op args[5]
  14.3 0.1 pad_add_fusion.edge_ref
  14.4 0.0 collective-permute-done.left_ref
  14.4 0.9 collective-permute-done.1.right_ref
  15.4 3.1 %collective-permute-start.2 = (bf16[136,128]{1,0:T(8,128)(2,1)S(1)}, bf16[136,128]{1,0:T(8,128)(2,1)S(1)}, u32[]{:S(2)}, u32[]{:S(2)}) collective-permute-start(bf16[136,128]{1,0:T(8,128)(2,1)S(1)} %pad_maximum_fusion), channel_id=1, source_target_pairs={{0,16},{16,32},{32,48},{48,64},{64,80},{80,96},{96,112},{1,17},{17... | collective-permute-start | bytes 104456 | tf_op jit(solution)/shard_map/ppermute | solution.py:559
  18.5 1.3 collective-permute-start.3
  19.8 0.0 copy-done
  19.8 0.0 copy-done.3
  19.8 0.0 copy-done.2
  19.8 7.8 %front_inner.1 = bf16[16,4,2,8,512]{4,3,2,1,0:T(8,128)(2,1)} custom-call(s32[4]{0:T(128)S(1)} %pad_add_fusion.edge_ref, bf16[128,64,128]{2,1,0:T(8,128)(2,1)S(1)} %copy-done, bf16[2,128,128]{2,1,0:T(8,128)(2,1)S(1)} %collective-permute-done.left_ref, bf16[2,128,128]{2,1,0:T(8,128)(2,1)S(1)} %collective-permute-done.1.right_ref, ...), custom_call_target="tpu_custom_call" | custom-call | flops 8000000000 | bytes 5000000 | tf_op jit(solution)/shard_map/front_inner/pallas_call | solution.py:264
  27.6 0.0 collective-permute-done.2.rest_0_
  27.6 0.0 collective-permute-done.3.rest_1_
  27.7 0.1 broadcast_in_dim.2.qgain_ref
  27.8 10.3 %all-to-all-start.2 = ((bf16[128,8,512]{2,1,0:T(8,128)(2,1)}), bf16[128,8,512]{2,1,0:T(8,128)(2,1)S(1)}, u32[]{:S(2)}, u32[]{:S(2)}) async-start(bf16[128,8,512]{2,1,0:T(8,128)(2,1)} %bitcast.23), calls=%async_computation.2 | async-start | bytes 2097152 | tf_op jit(solution)/shard_map/all_to_all | solution.py:616
  38.1 8.7 %front_outer.1 = bf16[16,4,2,8,512]{4,3,2,1,0:T(8,128)(2,1)} custom-call(s32[4]{0:T(128)S(1)} %pad_add_fusion.edge_ref, bf16[128,64,128]{2,1,0:T(8,128)(2,1)} %x_hbm.3, bf16[2,128,128]{2,1,0:T(8,128)(2,1)S(1)} %collective-permute-done.left_ref, bf16[2,128,128]{2,1,0:T(8,128)(2,1)S(1)} %collective-permute-done.1.right_ref, ...), custom_call_target="tpu_custom_call" | custom-call | flops 8000000000 | bytes 5000000 | tf_op jit(solution)/shard_map/front_outer/pallas_call | solution.py:264
  46.8 0.0 copy-start.1
  46.8 10.2 %all-to-all-done.2.tok_ref = bf16[128,8,512]{2,1,0:T(8,128)(2,1)S(1)} async-done(((bf16[128,8,512]{2,1,0:T(8,128)(2,1)}), bf16[128,8,512]{2,1,0:T(8,128)(2,1)S(1)}, u32[]{:S(2)}, u32[]{:S(2)}) %all-to-all-start.2) | async-done | bytes 1048608 | tf_op jit(solution)/shard_map/all_to_all | solution.py:616
  57.0 4.8 %all-to-all-start = ((bf16[128,8,512]{2,1,0:T(8,128)(2,1)}), bf16[128,8,512]{2,1,0:T(8,128)(2,1)S(1)}, u32[]{:S(2)}, u32[]{:S(2)}) async-start(bf16[128,8,512]{2,1,0:T(8,128)(2,1)} %bitcast.24), calls=%async_computation | async-start | bytes 2097152 | tf_op jit(solution)/shard_map/all_to_all | solution.py:620
  61.9 0.0 copy-done.1
  61.9 15.8 %middle.3 = bf16[128,8,512]{2,1,0:T(8,128)(2,1)} custom-call(bf16[128,8,512]{2,1,0:T(8,128)(2,1)S(1)} %all-to-all-done.2.tok_ref, f32[4,512]{1,0:T(4,128)S(1)} %copy-done.1, f32[512,128]{1,0:T(8,128)S(1)} %broadcast_in_dim.2.qgain_ref, bf16[1536,512]{1,0:T(8,128)(2,1)} %bitcast.21, bf16[512,512]{1,0:T(8,128)(2,1)} %wout_hbm.3, bf16[512,2048]{1,0:T(8,128)(2,1)} %wi_hbm.3, ...), custom_call_target="tpu_custom_call" | custom-call | flops 16000000000 | bytes 9000000 | tf_op jit(solution)/shard_map/middle/pallas_call | solution.py:439
  77.7 3.1 %all-to-all-done.tok_ref = bf16[128,8,512]{2,1,0:T(8,128)(2,1)S(1)} async-done(((bf16[128,8,512]{2,1,0:T(8,128)(2,1)}), bf16[128,8,512]{2,1,0:T(8,128)(2,1)S(1)}, u32[]{:S(2)}, u32[]{:S(2)}) %all-to-all-start) | async-done | bytes 1048608 | tf_op jit(solution)/shard_map/all_to_all | solution.py:620
  80.8 6.7 %all-to-all-start.3 = ((bf16[128,8,512]{2,1,0:T(8,128)(2,1)}), bf16[128,8,512]{2,1,0:T(8,128)(2,1)S(1)}, u32[]{:S(2)}, u32[]{:S(2)}) async-start(bf16[128,8,512]{2,1,0:T(8,128)(2,1)} %middle.3), calls=%async_computation.3 | async-start | bytes 2097152 | tf_op jit(solution)/shard_map/all_to_all | solution.py:624
  87.5 15.8 %middle.2 = bf16[128,8,512]{2,1,0:T(8,128)(2,1)} custom-call(bf16[128,8,512]{2,1,0:T(8,128)(2,1)S(1)} %all-to-all-done.tok_ref, f32[4,512]{1,0:T(4,128)S(1)} %copy-done.1, f32[512,128]{1,0:T(8,128)S(1)} %broadcast_in_dim.2.qgain_ref, bf16[1536,512]{1,0:T(8,128)(2,1)} %bitcast.22, bf16[512,512]{1,0:T(8,128)(2,1)} %wout_hbm.3, bf16[512,2048]{1,0:T(8,128)(2,1)} %wi_hbm.3, ...), custom_call_target="tpu_custom_call" | custom-call | flops 16000000000 | bytes 9000000 | tf_op jit(solution)/shard_map/middle/pallas_call | solution.py:439
  103.4 3.1 %all-to-all-done.3.refs_0_ = bf16[128,8,512]{2,1,0:T(8,128)(2,1)S(1)} async-done(((bf16[128,8,512]{2,1,0:T(8,128)(2,1)}), bf16[128,8,512]{2,1,0:T(8,128)(2,1)S(1)}, u32[]{:S(2)}, u32[]{:S(2)}) %all-to-all-start.3) | async-done | bytes 1048608 | tf_op jit(solution)/shard_map/all_to_all | solution.py:624
  106.4 6.7 %all-to-all-start.1 = ((bf16[128,8,512]{2,1,0:T(8,128)(2,1)}), bf16[128,8,512]{2,1,0:T(8,128)(2,1)S(1)}, u32[]{:S(2)}, u32[]{:S(2)}) async-start(bf16[128,8,512]{2,1,0:T(8,128)(2,1)} %middle.2), calls=%async_computation.1 | async-start | bytes 2097152 | tf_op jit(solution)/shard_map/all_to_all | solution.py:625
  113.1 3.5 %back_inner.1 = (bf16[2,64,64,128]{3,2,1,0:T(8,128)(2,1)}, bf16[2,2,16,64,128]{4,3,2,1,0:T(8,128)(2,1)S(1)}) custom-call(bf16[128,8,512]{2,1,0:T(8,128)(2,1)S(1)} %all-to-all-done.3.refs_0_, bf16[2,64,64,128]{3,2,1,0:T(8,128)(2,1)} %bitcast.20, bf16[512,512]{1,0:T(8,128)(2,1)} %refs_2_.3), custom_call_target="tpu_custom_call" | custom-call | flops 540000000 | bytes 4000000 | tf_op jit(solution)/shard_map/back_inner/pallas_call | solution.py:531
  116.6 15.4 %all-to-all-done.1.refs_0_ = bf16[128,8,512]{2,1,0:T(8,128)(2,1)S(1)} async-done(((bf16[128,8,512]{2,1,0:T(8,128)(2,1)}), bf16[128,8,512]{2,1,0:T(8,128)(2,1)S(1)}, u32[]{:S(2)}, u32[]{:S(2)}) %all-to-all-start.1) | async-done | bytes 1048608 | tf_op jit(solution)/shard_map/all_to_all | solution.py:625
  132.1 3.0 %back_outer.1 = bf16[2,64,64,128]{3,2,1,0:T(8,128)(2,1)} custom-call(bf16[128,8,512]{2,1,0:T(8,128)(2,1)S(1)} %all-to-all-done.1.refs_0_, bf16[2,2,16,64,128]{4,3,2,1,0:T(8,128)(2,1)S(1)} %get-tuple-element.17.refs_1_, bf16[512,512]{1,0:T(8,128)(2,1)} %refs_2_.3, bf16[2,64,64,128]{3,2,1,0:T(8,128)(2,1)} %get-tuple-element.18.refs_3_), custom_call_target="tpu_custom_call", output_to_operand_aliasing={{}: (3, {})} | custom-call | flops 540000000 | bytes 4000000 | tf_op jit(solution)/shard_map/back_outer/pallas_call | solution.py:531
  (6 shorter events, 0.1 us)
Async XLA Ops:
  0.0 19.8 %copy-start = (bf16[128,64,128]{2,1,0:T(8,128)(2,1)S(1)}, bf16[128,64,128]{2,1,0:T(8,128)(2,1)}, u32[]{:S(2)}) copy-start(bf16[128,64,128]{2,1,0:T(8,128)(2,1)} %x_hbm.3) | copy-start | bytes 6291460
  0.0 19.8 %copy-start.3 = (bf16[3,3,128,128]{3,2,1,0:T(8,128)(2,1)S(1)}, bf16[3,3,128,128]{3,2,1,0:T(8,128)(2,1)}, u32[]{:S(2)}) copy-start(bf16[3,3,128,128]{3,2,1,0:T(8,128)(2,1)} %rest_3_.1) | copy-start | bytes 884740
  0.0 19.8 %copy-start.2 = (bf16[3,3,128,128]{3,2,1,0:T(8,128)(2,1)S(1)}, bf16[3,3,128,128]{3,2,1,0:T(8,128)(2,1)}, u32[]{:S(2)}) copy-start(bf16[3,3,128,128]{3,2,1,0:T(8,128)(2,1)} %rest_2_.3) | copy-start | bytes 884740
  1.3 13.1 %collective-permute-start = (bf16[2,128,128]{2,1,0:T(8,128)(2,1)S(1)}, bf16[2,128,128]{2,1,0:T(8,128)(2,1)S(1)}, u32[]{:S(2)}, u32[]{:S(2)}) collective-permute-start(bf16[2,128,128]{2,1,0:T(8,128)(2,1)S(1)} %bitcast.27), channel_id=1, source_target_pairs={{0,1},{1,2},{2,3},{3,4},{4,5},{5,6},{6,7},{7,8},{8,9},{9,10},{10,1... | collective-permute-start | bytes 196616 | tf_op jit(solution)/shard_map/ppermute | solution.py:559
  8.2 7.1 %collective-permute-start.1 = (bf16[2,128,128]{2,1,0:T(8,128)(2,1)S(1)}, bf16[2,128,128]{2,1,0:T(8,128)(2,1)S(1)}, u32[]{:S(2)}, u32[]{:S(2)}) collective-permute-start(bf16[2,128,128]{2,1,0:T(8,128)(2,1)S(1)} %bitcast.28), channel_id=1, source_target_pairs={{1,0},{2,1},{3,2},{4,3},{5,4},{6,5},{7,6},{8,7},{9,8},{10,9},{11,1... | collective-permute-start | bytes 196616 | tf_op jit(solution)/shard_map/ppermute | solution.py:564
  15.4 12.3 %collective-permute-start.2 = (bf16[136,128]{1,0:T(8,128)(2,1)S(1)}, bf16[136,128]{1,0:T(8,128)(2,1)S(1)}, u32[]{:S(2)}, u32[]{:S(2)}) collective-permute-start(bf16[136,128]{1,0:T(8,128)(2,1)S(1)} %pad_maximum_fusion), channel_id=1, source_target_pairs={{0,16},{16,32},{32,48},{48,64},{64,80},{80,96},{96,112},{1,17},{17... | collective-permute-start | bytes 104456 | tf_op jit(solution)/shard_map/ppermute | solution.py:559
  18.5 9.1 %collective-permute-start.3 = (bf16[136,128]{1,0:T(8,128)(2,1)S(1)}, bf16[136,128]{1,0:T(8,128)(2,1)S(1)}, u32[]{:S(2)}, u32[]{:S(2)}) collective-permute-start(bf16[136,128]{1,0:T(8,128)(2,1)S(1)} %pad_maximum_fusion.1), channel_id=1, source_target_pairs={{16,0},{32,16},{48,32},{64,48},{80,64},{96,80},{112,96},{17,1},{33... | collective-permute-start | bytes 104456 | tf_op jit(solution)/shard_map/ppermute | solution.py:564
  27.8 29.2 %all-to-all-start.2 = ((bf16[128,8,512]{2,1,0:T(8,128)(2,1)}), bf16[128,8,512]{2,1,0:T(8,128)(2,1)S(1)}, u32[]{:S(2)}, u32[]{:S(2)}) async-start(bf16[128,8,512]{2,1,0:T(8,128)(2,1)} %bitcast.23), calls=%async_computation.2 | async-start | bytes 2097152 | tf_op jit(solution)/shard_map/all_to_all | solution.py:616
  46.8 15.0 %copy-start.1 = (f32[4,512]{1,0:T(4,128)S(1)}, f32[4,512]{1,0:T(4,128)}, u32[]{:S(2)}) copy-start(f32[4,512]{1,0:T(4,128)} %gains_ref.3) | copy-start | bytes 24580
  57.0 23.8 %all-to-all-start = ((bf16[128,8,512]{2,1,0:T(8,128)(2,1)}), bf16[128,8,512]{2,1,0:T(8,128)(2,1)S(1)}, u32[]{:S(2)}, u32[]{:S(2)}) async-start(bf16[128,8,512]{2,1,0:T(8,128)(2,1)} %bitcast.24), calls=%async_computation | async-start | bytes 2097152 | tf_op jit(solution)/shard_map/all_to_all | solution.py:620
  80.8 25.7 %all-to-all-start.3 = ((bf16[128,8,512]{2,1,0:T(8,128)(2,1)}), bf16[128,8,512]{2,1,0:T(8,128)(2,1)S(1)}, u32[]{:S(2)}, u32[]{:S(2)}) async-start(bf16[128,8,512]{2,1,0:T(8,128)(2,1)} %middle.3), calls=%async_computation.3 | async-start | bytes 2097152 | tf_op jit(solution)/shard_map/all_to_all | solution.py:624
  106.4 25.6 %all-to-all-start.1 = ((bf16[128,8,512]{2,1,0:T(8,128)(2,1)}), bf16[128,8,512]{2,1,0:T(8,128)(2,1)S(1)}, u32[]{:S(2)}, u32[]{:S(2)}) async-start(bf16[128,8,512]{2,1,0:T(8,128)(2,1)} %middle.2), calls=%async_computation.1 | async-start | bytes 2097152 | tf_op jit(solution)/shard_map/all_to_all | solution.py:625

commit v4 on v3

--- a/solution.py
+++ b/solution.py
@@ -458,7 +458,7 @@
     )(tokens, gains, qgain, win, wout, wi, wd)
 
 
-def back_cells(cells_ref, x_ref, we_ref, loads, out_ref, even, odd):
+def back_cells(cells_ref, x_ref, fill, we_ref, loads, out_ref, even, odd):
     cells = cells_ref[...].reshape(512, LATENT)
     for di, side in enumerate((even, odd)):
         if loads:
@@ -468,6 +468,7 @@
         )
         for dj in range(2):
             side[pl.ds(dj, 512, stride=2), :] = expanded[:, dj * CHANNELS : (dj + 1) * CHANNELS]
+    fill.wait()
     for di, side in enumerate((even, odd)):
         for u in range(8):
             rows = side[u * 128 : (u + 1) * 128, :].reshape(8, 2, 8, CHANNELS)
@@ -478,32 +479,31 @@
 
 
 def back_kernel(blocks, *refs):
-    we_ref, out_ref, even, odd, sems = refs[-5:]
-    expand = [
-        pltpu.make_async_copy(refs[2].at[:, lanes], we_ref.at[:, lanes], sems.at[q])
-        for q, lanes in enumerate((pl.ds(0, 256), pl.ds(256, 256)))
-    ]
-    for load in expand:
+    cells_ref, x_hbm, weight = refs[:3]
+    x_ref, we_ref, out_ref, even, odd, sems = refs[-6:]
+    out_hbm = refs[-7]
+    expand = []
+    if blocks == INNER:
+        expand = [
+            pltpu.make_async_copy(weight.at[:, lanes], we_ref.at[:, lanes], sems.at[q])
+            for q, lanes in enumerate((pl.ds(0, 256), pl.ds(256, 256)))
+        ]
+    else:
+        we_ref = weight
+    loads = [
+        pltpu.make_async_copy(
+            x_hbm.at[:, pl.ds(16 * block, 16)], x_ref.at[i], sems.at[4 + i]
+        )
+        for i, block in enumerate(blocks)
+    ]
+    for load in expand + loads:
         load.start()
-    if blocks == INNER:
-        cells_ref, x_hbm, we_hbm, out_hbm, kept, x_ref = refs[:6]
-        spans = [(x_hbm, INNER[0], x_ref.at[0]), (x_hbm, INNER[1], x_ref.at[1])]
-        spans += [(x_hbm, OUTER[0], kept.at[0]), (x_hbm, OUTER[1], kept.at[1])]
-        loads = [
-            pltpu.make_async_copy(x.at[:, pl.ds(16 * block, 16)], to, sems.at[4 + i])
-            for i, (x, block, to) in enumerate(spans)
-        ]
-        for load in loads:
-            load.start()
-    else:
-        cells_ref, x_ref, we_hbm, _, out_hbm = refs[:5]
     stores = []
     for at, block in enumerate(blocks):
-        if blocks == INNER:
-            loads[at].wait()
         back_cells(
             cells_ref.at[pl.ds(64 * at, 64)],
             x_ref.at[at],
+            loads[at],
             we_ref,
             expand if at == 0 else (),
             out_ref.at[at],
@@ -517,9 +517,6 @@
         stores.append(store)
     for store in stores:
         store.wait()
-    if blocks == INNER:
-        loads[2].wait()
-        loads[3].wait()
 
 
 def back(blocks, cells, *others):
@@ -530,16 +527,16 @@
     first = blocks == INNER
     return pl.pallas_call(
         functools.partial(back_kernel, blocks),
-        out_shape=(field, part) if first else field,
-        in_specs=[vmem, hbm, hbm] if first else [vmem, vmem, hbm, hbm],
-        out_specs=(hbm, vmem) if first else hbm,
-        scratch_shapes=([part] if first else [])
-        + [
+        out_shape=field,
+        in_specs=[vmem, hbm, hbm] if first else [vmem, hbm, vmem, hbm],
+        out_specs=hbm,
+        scratch_shapes=[
+            part,
             pltpu.VMEM((LATENT, LATENT), jnp.bfloat16),
             part,
             pltpu.VMEM((1024, CHANNELS), jnp.float32),
             pltpu.VMEM((1024, CHANNELS), jnp.float32),
-            pltpu.SemaphoreType.DMA((8 if first else 4,)),
+            pltpu.SemaphoreType.DMA((6,)),
         ],
         input_output_aliases={} if first else {3: 0},
         compiler_params=pltpu.CompilerParams(vmem_limit_bytes=16 << 20),
@@ -624,9 +621,8 @@
     inner = exchange(middle(inner, *weights))
     outer = exchange(middle(outer, *weights))
     field = held(x.reshape(2, 64, COLS, CHANNELS))
-    expand = held(expand_weight)
-    result, rest = back(INNER, inner, field, expand)
-    result = back(OUTER, outer, rest, expand, result)
+    result = back(INNER, inner, field, held(expand_weight))
+    result = back(OUTER, outer, field, expand_weight, result)
     return result.reshape(ROWS, COLS, CHANNELS)
 
 

time: 136 us -> 135 us (level)
  no operation moved by 1% of the time
where the time goes in v4:
time: 135 us
  Pallas kernels  53.9 us (40%)
  starting transfers between devices  41.8 us (31%)
  waiting for transfers between devices  32.9 us (24%)
  local copies, waits for them, and re-layouts  4.84 us (4%)
    pallas_call x2, Pallas kernels, middle(): pl.pallas_call(middle_kernel, out_shape=pltpu.HBM((128, 8, LATENT), jnp.b...  31.7 us
    pallas_call x2, Pallas kernels, front(): pl.pallas_call(functools.partial(front_kernel, blocks), out_shape=pltpu.H...  16.5 us
    all_to_all x1, waiting for transfers between devices, per_device(): outer = exchange(middle(outer, *weights))  15.7 us
    all_to_all x1, starting transfers between devices, per_device(): inner = exchange(inner)  10.3 us
    all_to_all x1, waiting for transfers between devices, per_device(): inner = exchange(inner)  10.2 us
    ppermute x2, starting transfers between devices, from_before(): return lax.ppermute(cells, axis, [(i, i + 1) for i in range(ends)])  10 us
    all_to_all x1, starting transfers between devices, per_device(): inner = exchange(middle(inner, *weights))  6.72 us
    all_to_all x1, starting transfers between devices, per_device(): outer = exchange(middle(outer, *weights))  6.7 us
  transfers between devices with their start and end apart: 8, of which 5 were waited for; matrix products, arithmetic and copies ran while one was open for 3% of the time, Pallas kernels for 38%

profile of v4, /device:TPU:1, one launch (start us, length us, event | category | flops | bytes accessed | tf_op | source)
XLA Modules:
  0.0 134.7 jit_solution(17042293052847229196)
XLA Ops:
  0.0 0.0 copy-start
  0.0 0.0 copy-start.4
  0.0 0.0 copy-start.3
  0.0 1.3 fusion.1
  1.3 6.9 %collective-permute-start = (bf16[2,128,128]{2,1,0:T(8,128)(2,1)S(1)}, bf16[2,128,128]{2,1,0:T(8,128)(2,1)S(1)}, u32[]{:S(2)}, u32[]{:S(2)}) collective-permute-start(bf16[2,128,128]{2,1,0:T(8,128)(2,1)S(1)} %bitcast.28), channel_id=1, source_target_pairs={{0,1},{1,2},{2,3},{3,4},{4,5},{5,6},{6,7},{7,8},{8,9},{9,10},{10,1... | collective-permute-start | bytes 196616 | tf_op jit(solution)/shard_map/ppermute | solution.py:556
  8.2 1.9 %collective-permute-start.1 = (bf16[2,128,128]{2,1,0:T(8,128)(2,1)S(1)}, bf16[2,128,128]{2,1,0:T(8,128)(2,1)S(1)}, u32[]{:S(2)}, u32[]{:S(2)}) collective-permute-start(bf16[2,128,128]{2,1,0:T(8,128)(2,1)S(1)} %bitcast.29), channel_id=1, source_target_pairs={{1,0},{2,1},{3,2},{4,3},{5,4},{6,5},{7,6},{8,7},{9,8},{10,9},{11,1... | collective-permute-start | bytes 196616 | tf_op jit(solution)/shard_map/ppermute | solution.py:561
  10.2 0.8 fusion
  11.0 0.8 multiply_multiply_fusion
  11.7 2.6 %copy.14 = bf16[512,1536]{0,1:T(8,128)(2,1)} copy(bf16[512,1536]{1,0:T(8,128)(2,1)} %param.15) | data formatting | bytes 3145728 | tf_op args[5]
  14.3 0.1 pad_add_fusion.edge_ref
  14.4 0.0 collective-permute-done.left_ref
  14.4 0.9 collective-permute-done.1.right_ref
  15.4 3.1 %collective-permute-start.2 = (bf16[136,128]{1,0:T(8,128)(2,1)S(1)}, bf16[136,128]{1,0:T(8,128)(2,1)S(1)}, u32[]{:S(2)}, u32[]{:S(2)}) collective-permute-start(bf16[136,128]{1,0:T(8,128)(2,1)S(1)} %pad_maximum_fusion), channel_id=1, source_target_pairs={{0,16},{16,32},{32,48},{48,64},{64,80},{80,96},{96,112},{1,17},{17... | collective-permute-start | bytes 104456 | tf_op jit(solution)/shard_map/ppermute | solution.py:556
  18.5 1.3 collective-permute-start.3
  19.8 0.0 copy-done
  19.8 0.0 copy-done.4
  19.8 0.0 copy-done.3
  19.8 7.8 %front_inner.1 = bf16[16,4,2,8,512]{4,3,2,1,0:T(8,128)(2,1)} custom-call(s32[4]{0:T(128)S(1)} %pad_add_fusion.edge_ref, bf16[128,64,128]{2,1,0:T(8,128)(2,1)S(1)} %copy-done, bf16[2,128,128]{2,1,0:T(8,128)(2,1)S(1)} %collective-permute-done.left_ref, bf16[2,128,128]{2,1,0:T(8,128)(2,1)S(1)} %collective-permute-done.1.right_ref, ...), custom_call_target="tpu_custom_call" | custom-call | flops 8000000000 | bytes 5000000 | tf_op jit(solution)/shard_map/front_inner/pallas_call | solution.py:264
  27.6 0.0 collective-permute-done.2.rest_0_
  27.6 0.0 collective-permute-done.3.rest_1_
  27.6 0.1 broadcast_in_dim.2.qgain_ref
  27.8 10.3 %all-to-all-start.2 = ((bf16[128,8,512]{2,1,0:T(8,128)(2,1)}), bf16[128,8,512]{2,1,0:T(8,128)(2,1)S(1)}, u32[]{:S(2)}, u32[]{:S(2)}) async-start(bf16[128,8,512]{2,1,0:T(8,128)(2,1)} %bitcast.24), calls=%async_computation.2 | async-start | bytes 2097152 | tf_op jit(solution)/shard_map/all_to_all | solution.py:613
  38.1 8.7 %front_outer.1 = bf16[16,4,2,8,512]{4,3,2,1,0:T(8,128)(2,1)} custom-call(s32[4]{0:T(128)S(1)} %pad_add_fusion.edge_ref, bf16[128,64,128]{2,1,0:T(8,128)(2,1)} %x_hbm.3, bf16[2,128,128]{2,1,0:T(8,128)(2,1)S(1)} %collective-permute-done.left_ref, bf16[2,128,128]{2,1,0:T(8,128)(2,1)S(1)} %collective-permute-done.1.right_ref, ...), custom_call_target="tpu_custom_call" | custom-call | flops 8000000000 | bytes 5000000 | tf_op jit(solution)/shard_map/front_outer/pallas_call | solution.py:264
  46.8 0.0 copy-start.2
  46.8 10.2 %all-to-all-done.2.tok_ref = bf16[128,8,512]{2,1,0:T(8,128)(2,1)S(1)} async-done(((bf16[128,8,512]{2,1,0:T(8,128)(2,1)}), bf16[128,8,512]{2,1,0:T(8,128)(2,1)S(1)}, u32[]{:S(2)}, u32[]{:S(2)}) %all-to-all-start.2) | async-done | bytes 1048608 | tf_op jit(solution)/shard_map/all_to_all | solution.py:613
  57.0 4.8 %all-to-all-start = ((bf16[128,8,512]{2,1,0:T(8,128)(2,1)}), bf16[128,8,512]{2,1,0:T(8,128)(2,1)S(1)}, u32[]{:S(2)}, u32[]{:S(2)}) async-start(bf16[128,8,512]{2,1,0:T(8,128)(2,1)} %bitcast.25), calls=%async_computation | async-start | bytes 2097152 | tf_op jit(solution)/shard_map/all_to_all | solution.py:617
  61.8 0.0 copy-done.2
  61.8 15.9 %middle.3 = bf16[128,8,512]{2,1,0:T(8,128)(2,1)} custom-call(bf16[128,8,512]{2,1,0:T(8,128)(2,1)S(1)} %all-to-all-done.2.tok_ref, f32[4,512]{1,0:T(4,128)S(1)} %copy-done.2, f32[512,128]{1,0:T(8,128)S(1)} %broadcast_in_dim.2.qgain_ref, bf16[1536,512]{1,0:T(8,128)(2,1)} %bitcast.22, bf16[512,512]{1,0:T(8,128)(2,1)} %wout_hbm.3, bf16[512,2048]{1,0:T(8,128)(2,1)} %wi_hbm.3, ...), custom_call_target="tpu_custom_call" | custom-call | flops 16000000000 | bytes 9000000 | tf_op jit(solution)/shard_map/middle/pallas_call | solution.py:439
  77.7 3.1 %all-to-all-done.tok_ref = bf16[128,8,512]{2,1,0:T(8,128)(2,1)S(1)} async-done(((bf16[128,8,512]{2,1,0:T(8,128)(2,1)}), bf16[128,8,512]{2,1,0:T(8,128)(2,1)S(1)}, u32[]{:S(2)}, u32[]{:S(2)}) %all-to-all-start) | async-done | bytes 1048608 | tf_op jit(solution)/shard_map/all_to_all | solution.py:617
  80.8 6.7 %all-to-all-start.3 = ((bf16[128,8,512]{2,1,0:T(8,128)(2,1)}), bf16[128,8,512]{2,1,0:T(8,128)(2,1)S(1)}, u32[]{:S(2)}, u32[]{:S(2)}) async-start(bf16[128,8,512]{2,1,0:T(8,128)(2,1)} %middle.3), calls=%async_computation.3 | async-start | bytes 2097152 | tf_op jit(solution)/shard_map/all_to_all | solution.py:621
  87.5 15.8 %middle.2 = bf16[128,8,512]{2,1,0:T(8,128)(2,1)} custom-call(bf16[128,8,512]{2,1,0:T(8,128)(2,1)S(1)} %all-to-all-done.tok_ref, f32[4,512]{1,0:T(4,128)S(1)} %copy-done.2, f32[512,128]{1,0:T(8,128)S(1)} %broadcast_in_dim.2.qgain_ref, bf16[1536,512]{1,0:T(8,128)(2,1)} %bitcast.23, bf16[512,512]{1,0:T(8,128)(2,1)} %wout_hbm.3, bf16[512,2048]{1,0:T(8,128)(2,1)} %wi_hbm.3, ...), custom_call_target="tpu_custom_call" | custom-call | flops 16000000000 | bytes 9000000 | tf_op jit(solution)/shard_map/middle/pallas_call | solution.py:439
  103.3 3.1 %all-to-all-done.3.refs_0_ = bf16[128,8,512]{2,1,0:T(8,128)(2,1)S(1)} async-done(((bf16[128,8,512]{2,1,0:T(8,128)(2,1)}), bf16[128,8,512]{2,1,0:T(8,128)(2,1)S(1)}, u32[]{:S(2)}, u32[]{:S(2)}) %all-to-all-start.3) | async-done | bytes 1048608 | tf_op jit(solution)/shard_map/all_to_all | solution.py:621
  106.4 6.7 %all-to-all-start.1 = ((bf16[128,8,512]{2,1,0:T(8,128)(2,1)}), bf16[128,8,512]{2,1,0:T(8,128)(2,1)S(1)}, u32[]{:S(2)}, u32[]{:S(2)}) async-start(bf16[128,8,512]{2,1,0:T(8,128)(2,1)} %middle.2), calls=%async_computation.1 | async-start | bytes 2097152 | tf_op jit(solution)/shard_map/all_to_all | solution.py:622
  113.1 0.0 copy-start.1
  113.1 3.2 %back_inner.1.refs_3_ = bf16[2,64,64,128]{3,2,1,0:T(8,128)(2,1)} custom-call(bf16[128,8,512]{2,1,0:T(8,128)(2,1)S(1)} %all-to-all-done.3.refs_0_, bf16[2,64,64,128]{3,2,1,0:T(8,128)(2,1)} %bitcast.20, bf16[512,512]{1,0:T(8,128)(2,1)} %refs_2_.3), custom_call_target="tpu_custom_call" | custom-call | flops 540000000 | bytes 4000000 | tf_op jit(solution)/shard_map/back_inner/pallas_call | solution.py:528
  116.4 15.7 %all-to-all-done.1.refs_0_ = bf16[128,8,512]{2,1,0:T(8,128)(2,1)S(1)} async-done(((bf16[128,8,512]{2,1,0:T(8,128)(2,1)}), bf16[128,8,512]{2,1,0:T(8,128)(2,1)S(1)}, u32[]{:S(2)}, u32[]{:S(2)}) %all-to-all-start.1) | async-done | bytes 1048608 | tf_op jit(solution)/shard_map/all_to_all | solution.py:622
  132.0 0.0 copy-done.1
  132.0 2.4 %back_outer.1 = bf16[2,64,64,128]{3,2,1,0:T(8,128)(2,1)} custom-call(bf16[128,8,512]{2,1,0:T(8,128)(2,1)S(1)} %all-to-all-done.1.refs_0_, bf16[2,64,64,128]{3,2,1,0:T(8,128)(2,1)} %bitcast.21, bf16[512,512]{1,0:T(8,128)(2,1)S(1)} %copy-done.1, bf16[2,64,64,128]{3,2,1,0:T(8,128)(2,1)} %back_inner.1.refs_3_), custom_call_target="tpu_custom_call", output_to_operand_aliasing={{}: (3, {})} | custom-call | flops 540000000 | bytes 4000000 | tf_op jit(solution)/shard_map/back_outer/pallas_call | solution.py:528
  (6 shorter events, 0.1 us)
Async XLA Ops:
  0.0 19.8 %copy-start = (bf16[128,64,128]{2,1,0:T(8,128)(2,1)S(1)}, bf16[128,64,128]{2,1,0:T(8,128)(2,1)}, u32[]{:S(2)}) copy-start(bf16[128,64,128]{2,1,0:T(8,128)(2,1)} %x_hbm.3) | copy-start | bytes 6291460
  0.0 19.8 %copy-start.4 = (bf16[3,3,128,128]{3,2,1,0:T(8,128)(2,1)S(1)}, bf16[3,3,128,128]{3,2,1,0:T(8,128)(2,1)}, u32[]{:S(2)}) copy-start(bf16[3,3,128,128]{3,2,1,0:T(8,128)(2,1)} %rest_3_.1) | copy-start | bytes 884740
  0.0 19.8 %copy-start.3 = (bf16[3,3,128,128]{3,2,1,0:T(8,128)(2,1)S(1)}, bf16[3,3,128,128]{3,2,1,0:T(8,128)(2,1)}, u32[]{:S(2)}) copy-start(bf16[3,3,128,128]{3,2,1,0:T(8,128)(2,1)} %rest_2_.3) | copy-start | bytes 884740
  1.3 13.1 %collective-permute-start = (bf16[2,128,128]{2,1,0:T(8,128)(2,1)S(1)}, bf16[2,128,128]{2,1,0:T(8,128)(2,1)S(1)}, u32[]{:S(2)}, u32[]{:S(2)}) collective-permute-start(bf16[2,128,128]{2,1,0:T(8,128)(2,1)S(1)} %bitcast.28), channel_id=1, source_target_pairs={{0,1},{1,2},{2,3},{3,4},{4,5},{5,6},{6,7},{7,8},{8,9},{9,10},{10,1... | collective-permute-start | bytes 196616 | tf_op jit(solution)/shard_map/ppermute | solution.py:556
  8.2 7.1 %collective-permute-start.1 = (bf16[2,128,128]{2,1,0:T(8,128)(2,1)S(1)}, bf16[2,128,128]{2,1,0:T(8,128)(2,1)S(1)}, u32[]{:S(2)}, u32[]{:S(2)}) collective-permute-start(bf16[2,128,128]{2,1,0:T(8,128)(2,1)S(1)} %bitcast.29), channel_id=1, source_target_pairs={{1,0},{2,1},{3,2},{4,3},{5,4},{6,5},{7,6},{8,7},{9,8},{10,9},{11,1... | collective-permute-start | bytes 196616 | tf_op jit(solution)/shard_map/ppermute | solution.py:561
  15.4 12.3 %collective-permute-start.2 = (bf16[136,128]{1,0:T(8,128)(2,1)S(1)}, bf16[136,128]{1,0:T(8,128)(2,1)S(1)}, u32[]{:S(2)}, u32[]{:S(2)}) collective-permute-start(bf16[136,128]{1,0:T(8,128)(2,1)S(1)} %pad_maximum_fusion), channel_id=1, source_target_pairs={{0,16},{16,32},{32,48},{48,64},{64,80},{80,96},{96,112},{1,17},{17... | collective-permute-start | bytes 104456 | tf_op jit(solution)/shard_map/ppermute | solution.py:556
  18.5 9.1 %collective-permute-start.3 = (bf16[136,128]{1,0:T(8,128)(2,1)S(1)}, bf16[136,128]{1,0:T(8,128)(2,1)S(1)}, u32[]{:S(2)}, u32[]{:S(2)}) collective-permute-start(bf16[136,128]{1,0:T(8,128)(2,1)S(1)} %pad_maximum_fusion.1), channel_id=1, source_target_pairs={{16,0},{32,16},{48,32},{64,48},{80,64},{96,80},{112,96},{17,1},{33... | collective-permute-start | bytes 104456 | tf_op jit(solution)/shard_map/ppermute | solution.py:561
  27.8 29.2 %all-to-all-start.2 = ((bf16[128,8,512]{2,1,0:T(8,128)(2,1)}), bf16[128,8,512]{2,1,0:T(8,128)(2,1)S(1)}, u32[]{:S(2)}, u32[]{:S(2)}) async-start(bf16[128,8,512]{2,1,0:T(8,128)(2,1)} %bitcast.24), calls=%async_computation.2 | async-start | bytes 2097152 | tf_op jit(solution)/shard_map/all_to_all | solution.py:613
  46.8 15.0 %copy-start.2 = (f32[4,512]{1,0:T(4,128)S(1)}, f32[4,512]{1,0:T(4,128)}, u32[]{:S(2)}) copy-start(f32[4,512]{1,0:T(4,128)} %gains_ref.3) | copy-start | bytes 24580
  57.0 23.8 %all-to-all-start = ((bf16[128,8,512]{2,1,0:T(8,128)(2,1)}), bf16[128,8,512]{2,1,0:T(8,128)(2,1)S(1)}, u32[]{:S(2)}, u32[]{:S(2)}) async-start(bf16[128,8,512]{2,1,0:T(8,128)(2,1)} %bitcast.25), calls=%async_computation | async-start | bytes 2097152 | tf_op jit(solution)/shard_map/all_to_all | solution.py:617
  80.8 25.6 %all-to-all-start.3 = ((bf16[128,8,512]{2,1,0:T(8,128)(2,1)}), bf16[128,8,512]{2,1,0:T(8,128)(2,1)S(1)}, u32[]{:S(2)}, u32[]{:S(2)}) async-start(bf16[128,8,512]{2,1,0:T(8,128)(2,1)} %middle.3), calls=%async_computation.3 | async-start | bytes 2097152 | tf_op jit(solution)/shard_map/all_to_all | solution.py:621
  106.4 25.6 %all-to-all-start.1 = ((bf16[128,8,512]{2,1,0:T(8,128)(2,1)}), bf16[128,8,512]{2,1,0:T(8,128)(2,1)S(1)}, u32[]{:S(2)}, u32[]{:S(2)}) async-start(bf16[128,8,512]{2,1,0:T(8,128)(2,1)} %middle.2), calls=%async_computation.1 | async-start | bytes 2097152 | tf_op jit(solution)/shard_map/all_to_all | solution.py:622
  113.1 18.9 %copy-start.1 = (bf16[512,512]{1,0:T(8,128)(2,1)S(1)}, bf16[512,512]{1,0:T(8,128)(2,1)}, u32[]{:S(2)}) copy-start(bf16[512,512]{1,0:T(8,128)(2,1)} %refs_2_.3) | copy-start | bytes 1572868
